TPU v7x, 256 devices: a whole 4x4x8 slice. The times are simulated.
256 devices in a mesh: gx: 128 (over y, z_lo, x, core), gy: 2 (over z_hi).
Axes of the slice: x: 4, y: 4, z: 8 (z_hi: 2, z_lo: 4; z = z_hi * 4 + z_lo), core: 2. Of those that a mesh axis runs over, the one named last changes fastest.
Arguments:
- coefficients: float32 [2, 16, 256, 256], P(None, None, 'gx'), may hold values from -6 to 6
- first_axis_basis: float32 [4096, 256], replicated, may hold values from -0.375 to 0.375
- basis_y: float32 [256, 256], P('gy'), may hold values from -0.375 to 0.375
- basis_z: float32 [32, 16], replicated, may hold values from -1.5 to 1.5
- conductivity: float32 [32, 4096, 256], P(None, 'gx', 'gy'), may hold values from 0.3 to 3
- pressure: float32 [32, 4096, 256], P(None, 'gx', 'gy'), may hold values from -6 to 6
Outputs:
- hess_action: float32 [2, 16, 256, 256], P(None, None, 'gx', 'gy')
All inputs are finite; a program needn't handle non-finite values.
Results may differ from a plain program's by a relative error of at most 0.000067.
Values sent between devices are 32-bit elements; how exact they have to be, the bound alone decides.
No kernel may reach another device: no remote copies, remote signals or barrier semaphores. Data moves between devices by JAX's collectives and lax.ppermute only.
A program may use at most 128 MiB of HBM per device.

v0:
```python
import jax
import jax.numpy as jnp
from jax import lax
from jax.experimental import pallas as pl
from jax.experimental.pallas import tpu as pltpu
from jax.sharding import Mesh, PartitionSpec as P

step_size = 0.05
highest = lax.Precision.HIGHEST
f32 = jnp.float32

AXES = ("y", "zl", "x", "core", "zh")
SIZES = (4, 4, 4, 2, 2)
GX = ("y", "zl", "x", "core")
PLANE = ("y", "x", "core")
RING = ("zl", "zh")

DIRECTIONS, MODES_Z, DEPTH = 2, 16, 32
ROWS, COLS = 32, 128
HALO = 4
EXT_ROWS = ROWS + 2 * HALO
EXT_COLS = 2 * COLS
STRIP = 8
GROUPS = EXT_ROWS // STRIP
MODES = 256
BLOCK = 8 * ROWS
VMEM = pl.BlockSpec(memory_space=pltpu.VMEM)
SMEM = pl.BlockSpec(memory_space=pltpu.SMEM)
ANY = pl.BlockSpec(memory_space=pl.ANY)


def params():
    return pltpu.CompilerParams(vmem_limit_bytes=48 * 1024 * 1024)


def pack_kernel(where, kap, prs, upper, lower, rows_out, strip_out):
    zh = where[1]
    lane = lax.broadcasted_iota(jnp.int32, (STRIP, COLS), 1)

    def body(z, carry):
        packed = jnp.zeros((STRIP, COLS), f32)
        for f, ref in enumerate((kap, prs)):
            beside = jnp.concatenate([upper[f, z], lower[f, z]], axis=0)
            rows_out[f, z] = beside
            for g in range(GROUPS):
                tile = ref[z, pl.ds(8 * g, 8)] if g < ROWS // 8 else beside
                first = f * EXT_ROWS + 8 * g
                shift = lax.rem(first + 8 * (1 - zh), COLS)
                moved = pltpu.roll(tile, shift, 1)
                packed = jnp.where((lane >= first) & (lane < first + 8), moved, packed)
        strip_out[z] = packed
        return carry

    lax.fori_loop(0, DEPTH, body, 0)


def pack(where, kap, prs, upper, lower):
    return pl.pallas_call(
        pack_kernel,
        out_shape=(
            jax.ShapeDtypeStruct((2, DEPTH, 2 * HALO, COLS), f32),
            jax.ShapeDtypeStruct((DEPTH, STRIP, COLS), f32),
        ),
        in_specs=[SMEM] + [VMEM] * 4,
        out_specs=(VMEM, VMEM),
        compiler_params=params(),
        cost_estimate=pl.CostEstimate(flops=2_000_000, bytes_accessed=1_600_000, transcendentals=0),
        name="pack",
    )(where, kap, prs, upper, lower)


def expand_kernel(where, coefs, basis, beside, first_basis, out, wide, blocks, sems):
    zl = where[2]
    copies = []
    for y in range(4):
        start = pl.multiple_of((y * 4 + zl) * BLOCK, BLOCK)
        below = pl.multiple_of(jnp.maximum(start - 8, 0), 8)
        above = pl.multiple_of(jnp.minimum(start + BLOCK, 4096 - 8), 8)
        for part, (src, size, dst) in enumerate(
            ((below, 8, 0), (start, BLOCK, 8), (above, 8, BLOCK + 8))
        ):
            copies.append(
                pltpu.make_async_copy(
                    first_basis.at[pl.ds(src, size)],
                    blocks.at[y, pl.ds(dst, size)],
                    sems.at[y, part],
                )
            )
    for copy in copies:
        copy.start()
    wide[pl.ds(0, COLS)] = basis[...]
    wide[pl.ds(COLS, STRIP)] = beside[...]
    wide[pl.ds(COLS + STRIP, COLS - STRIP)] = jnp.zeros((COLS - STRIP, MODES), f32)
    columns = lax.dot_general(
        coefs[...], wide[...], (((1,), (1,)), ((), ())),
        precision=highest, preferred_element_type=f32,
    )
    lane = lax.broadcasted_iota(jnp.int32, (STRIP, COLS), 1)
    low = lax.broadcasted_iota(jnp.int32, (STRIP, EXT_COLS), 0) < HALO
    for copy in copies:
        copy.wait()
    for y in range(4):
        full = lax.dot_general(
            blocks[y], columns, (((1,), (0,)), ((), ())),
            precision=highest, preferred_element_type=f32,
        )
        for k in range(8):
            own = full[8 + ROWS * k : 8 + ROWS * (k + 1)]
            above = full[8 + ROWS * (k + 1) : 16 + ROWS * (k + 1)]
            below = full[ROWS * k : ROWS * k + 8]
            ends = jnp.where(low, above, below)
            q = y * 8 + k
            out[q, pl.ds(0, ROWS)] = own[:, :COLS]
            out[q, pl.ds(ROWS, 8)] = ends[:, :COLS]
            packed = own[:8, COLS:]
            for g in range(1, GROUPS):
                tile = (own[8 * g : 8 * g + 8] if g < ROWS // 8 else ends)[:, COLS:]
                packed = jnp.where(lane < 8 * g, packed, pltpu.roll(tile, 8 * g, 1))
            out[q, pl.ds(EXT_ROWS, STRIP)] = packed


def expand(where, coefs, basis, beside, first_basis):
    return pl.pallas_call(
        expand_kernel,
        out_shape=jax.ShapeDtypeStruct((32, EXT_ROWS + STRIP, COLS), f32),
        in_specs=[SMEM, VMEM, VMEM, VMEM, ANY],
        out_specs=VMEM,
        scratch_shapes=[
            pltpu.VMEM((EXT_COLS, MODES), f32),
            pltpu.VMEM((4, BLOCK + 16, MODES), f32),
            pltpu.SemaphoreType.DMA((4, 3)),
        ],
        compiler_params=params(),
        cost_estimate=pl.CostEstimate(
            flops=6 * 2 * 256 * 256 * 1344, bytes_accessed=3_000_000, transcendentals=0
        ),
        name="expand",
    )(where, coefs, basis, beside, first_basis)


def grid_kernel(
    where, basis_z, layers, kap, prs, rows, strip, out,
    kk, pp, ex, ey, ez, px, py, pz, field, sens,
):
    gx, zh = where[0], where[1]
    row = lax.broadcasted_iota(jnp.int32, (EXT_ROWS, EXT_COLS), 0)
    col = lax.broadcasted_iota(jnp.int32, (EXT_ROWS, EXT_COLS), 1)
    no_x = ((row == ROWS - 1) & (gx == 127)) | ((row == EXT_ROWS - 1) & (gx == 0))
    no_y = ((col == COLS - 1) & (zh == 1)) | ((col == EXT_COLS - 1) & (zh == 0))
    mask_x = jnp.where(no_x, 0.0, 1.0).astype(f32)
    mask_y = jnp.where(no_y, 0.0, 1.0).astype(f32)
    core = pl.ds(0, COLS)
    side = pl.ds(COLS, COLS)

    def shift_of(lane):
        return lax.rem(120 * zh + 2 * COLS - lane, COLS)

    def x_next(v):
        return pltpu.roll(v, EXT_ROWS - 1, 0)

    def x_prev(v):
        return pltpu.roll(v, 1, 0)

    def y_next(v):
        return pltpu.roll(v, EXT_COLS - 1, 1)

    def y_prev(v):
        return pltpu.roll(v, 1, 1)

    def place(z, carry):
        for f, (src, dst) in enumerate(((kap, kk), (prs, pp))):
            dst[z, pl.ds(0, ROWS), core] = src[z]
            dst[z, pl.ds(ROWS, 8), core] = rows[f, z]
            packed = strip[z]
            for g in range(GROUPS):
                dst[z, pl.ds(8 * g, 8), side] = pltpu.roll(
                    packed, shift_of(f * EXT_ROWS + 8 * g), 1
                )
        return carry

    lax.fori_loop(0, DEPTH, place, 0)

    half = 0.5 * step_size * step_size

    def edges(z, carry):
        later = jnp.minimum(z + 1, DEPTH - 1)
        inside = jnp.where(z < DEPTH - 1, 1.0, 0.0).astype(f32)
        k, p = kk[z], pp[z]
        ex[z] = (half * mask_x) * (k + x_next(k))
        ey[z] = (half * mask_y) * (k + y_next(k))
        ez[z] = (half * inside) * (k + kk[later])
        px[z] = (0.5 * mask_x) * (x_next(p) - p)
        py[z] = (0.5 * mask_y) * (y_next(p) - p)
        pz[z] = (0.5 * inside) * (pp[later] - p)
        return carry

    lax.fori_loop(0, DEPTH, edges, 0)

    def layers_of(z, carry):
        for d in range(DIRECTIONS):
            total = basis_z[z, 0] * layers[d * MODES_Z]
            for c in range(1, MODES_Z):
                total = total + basis_z[z, c] * layers[d * MODES_Z + c]
            field[d, z, :, core] = kk[z, :, core] * total[:EXT_ROWS]
            packed = total[EXT_ROWS:]
            for g in range(GROUPS):
                at = pl.ds(8 * g, 8)
                field[d, z, at, side] = kk[z, at, side] * pltpu.roll(packed, shift_of(8 * g), 1)
        return carry

    lax.fori_loop(0, DEPTH, layers_of, 0)

    nothing = tuple(jnp.zeros((EXT_ROWS, EXT_COLS), f32) for _ in range(DIRECTIONS))

    def source_of(z, before):
        later = jnp.minimum(z + 1, DEPTH - 1)
        after = []
        for d in range(DIRECTIONS):
            c = field[d, z]
            fx = (c + x_next(c)) * px[z]
            fy = (c + y_next(c)) * py[z]
            fz = (c + field[d, later]) * pz[z]
            field[d, z] = (fx - x_prev(fx)) + (fy - y_prev(fy)) + (fz - before[d])
            after.append(fz)
        return tuple(after)

    lax.fori_loop(0, DEPTH, source_of, nothing)

    def advance(z, before):
        later = jnp.minimum(z + 1, DEPTH - 1)
        after = []
        for d in range(DIRECTIONS):
            u = field[d, z]
            fx = (x_next(u) - u) * ex[z]
            fy = (y_next(u) - u) * ey[z]
            fz = (field[d, later] - u) * ez[z]
            field[d, z] = (
                (2.0 * step_size) * u + (fx - x_prev(fx)) + (fy - y_prev(fy)) + (fz - before[d])
            )
            after.append(fz)
        return tuple(after)

    lax.fori_loop(0, DEPTH, advance, nothing)
    lax.fori_loop(0, DEPTH, advance, nothing)

    def couple(z, before):
        later = jnp.minimum(z + 1, DEPTH - 1)
        after = []
        for d in range(DIRECTIONS):
            w = field[d, z]
            fx = (x_next(w) - w) * px[z]
            fy = (y_next(w) - w) * py[z]
            fz = (field[d, later] - w) * pz[z]
            total = (fx + x_prev(fx)) + (fy + y_prev(fy)) + (fz + before[d])
            sens[d, z] = -kap[z] * total[:ROWS, :COLS]
            after.append(fz)
        return tuple(after)

    lax.fori_loop(0, DEPTH, couple, nothing)

    def modes_of(c, carry):
        for d in range(DIRECTIONS):
            total = basis_z[0, c] * sens[d, 0]
            for z in range(1, DEPTH):
                total = total + basis_z[z, c] * sens[d, z]
            out[d * MODES_Z + c] = total
        return carry

    lax.fori_loop(0, MODES_Z, modes_of, 0)


def on_grid(where, basis_z, layers, kap, prs, rows, strip):
    wide = (DEPTH, EXT_ROWS, EXT_COLS)
    return pl.pallas_call(
        grid_kernel,
        out_shape=jax.ShapeDtypeStruct((DIRECTIONS * MODES_Z, ROWS, COLS), f32),
        in_specs=[SMEM, SMEM] + [VMEM] * 5,
        out_specs=VMEM,
        scratch_shapes=[pltpu.VMEM(wide, f32) for _ in range(8)]
        + [
            pltpu.VMEM((DIRECTIONS,) + wide, f32),
            pltpu.VMEM((DIRECTIONS, DEPTH, ROWS, COLS), f32),
        ],
        compiler_params=params(),
        cost_estimate=pl.CostEstimate(
            flops=100_000_000, bytes_accessed=3_000_000, transcendentals=0
        ),
        name="on_grid",
    )(where, basis_z, layers, kap, prs, rows, strip)


def project_kernel(where, values, basis, first_basis, out, blocks, sems):
    zl = where[2]
    copies = []
    for y in range(4):
        start = pl.multiple_of((y * 4 + zl) * BLOCK, BLOCK)
        copies.append(
            pltpu.make_async_copy(
                first_basis.at[pl.ds(start, BLOCK)], blocks.at[pl.ds(y * BLOCK, BLOCK)], sems.at[y]
            )
        )
    for copy in copies:
        copy.start()
    for copy in copies:
        copy.wait()
    along_x = lax.dot_general(
        blocks[...], values[...], (((0,), (0,)), ((), ())),
        precision=highest, preferred_element_type=f32,
    )
    full = lax.dot_general(
        along_x, basis[...], (((1,), (0,)), ((), ())),
        precision=highest, preferred_element_type=f32,
    )
    for y in range(4):
        for z in range(4):
            at = y * 64 + z * 16
            for h in range(2):
                out[z * 2 + h, pl.ds(y * 16, 16)] = full[at : at + 16, h * 128 : (h + 1) * 128]


def project(where, values, basis, first_basis):
    return pl.pallas_call(
        project_kernel,
        out_shape=jax.ShapeDtypeStruct((8, 64, 128), f32),
        in_specs=[SMEM, VMEM, VMEM, ANY],
        out_specs=VMEM,
        scratch_shapes=[
            pltpu.VMEM((4 * BLOCK, MODES), f32),
            pltpu.SemaphoreType.DMA((4,)),
        ],
        compiler_params=params(),
        cost_estimate=pl.CostEstimate(
            flops=6 * 2 * 256 * 128 * 1280, bytes_accessed=2_000_000, transcendentals=0
        ),
        name="project",
    )(where, values, basis, first_basis)


def exchanged(values, axes):
    return lax.all_to_all(values, axes, split_axis=0, concat_axis=0, tiled=True)


def per_device(coefficients, first_axis_basis, basis_y, basis_z, conductivity, pressure):
    gx = lax.axis_index(GX)
    zh = lax.axis_index("zh")
    where = jnp.stack([gx, zh, lax.axis_index("zl")]).astype(jnp.int32)
    swap = [(0, 1), (1, 0)]

    flat = coefficients.reshape(DIRECTIONS * MODES_Z, 2, MODES)
    spread = jnp.broadcast_to(flat.reshape(4, 1, 8, 2, MODES), (4, 4, 8, 2, MODES))
    gathered = exchanged(spread.reshape(128, 2, MODES), GX)

    beside = lax.ppermute(
        lax.dynamic_slice_in_dim(basis_y, (COLS - STRIP) * (1 - zh), STRIP, 0), "zh", swap
    )
    statics = jnp.stack([conductivity, pressure])
    upper = lax.ppermute(statics[:, :, :HALO], GX, [((i + 1) % 128, i) for i in range(128)])
    lower = lax.ppermute(statics[:, :, -HALO:], GX, [(i, (i + 1) % 128) for i in range(128)])
    rows, strip = pack(where, conductivity, pressure, upper, lower)
    strip = lax.ppermute(strip, "zh", swap)

    message = expand(where, gathered.reshape(MODES, MODES), basis_y, beside, first_axis_basis)
    layers = exchanged(message, PLANE)
    modes = on_grid(where, basis_z, layers, conductivity, pressure, rows, strip)
    columns = exchanged(modes, PLANE)
    shares = project(where, columns.reshape(4 * BLOCK, COLS), basis_y, first_axis_basis)
    summed = jnp.sum(exchanged(shares, RING), axis=0)
    result = exchanged(summed.reshape(32, 2, 128), PLANE)
    own = lax.dynamic_slice_in_dim(coefficients, zh * 128, 128, 3)
    return result.reshape(DIRECTIONS, MODES_Z, 2, 128) + own


def solution(mesh):
    split = Mesh(mesh.devices.reshape(SIZES), AXES)
    return jax.shard_map(
        per_device,
        mesh=split,
        in_specs=(
            P(None, None, GX, None),
            P(),
            P("zh", None),
            P(),
            P(None, GX, "zh"),
            P(None, GX, "zh"),
        ),
        out_specs=P(None, None, GX, "zh"),
        check_vma=False,
    )
```

profile of v0, /device:TPU:33, one launch (start us, length us, event | category | flops | bytes accessed | tf_op | source)
XLA Modules:
  0.0 152.9 jit_solution(16425214377783928578)
XLA Ops:
  0.0 0.0 copy-start.2
  0.0 0.0 copy-start.3
  0.0 1.7 %broadcast_in_dim.8 = f32[4,4,8,2,256]{4,3,2,1,0:T(2,128)} broadcast(f32[4,8,2,256]{3,2,1,0:T(2,128)} %bitcast.13), dimensions={0,2,3,4} | broadcast | bytes 327680 | tf_op jit(solution)/shard_map/broadcast_in_dim | solution.py:350
  1.7 12.8 %all-to-all-start = ((f32[128,2,256]{2,1,0:T(2,128)}), f32[128,2,256]{2,1,0:T(2,128)S(1)}, u32[]{:S(2)}, u32[]{:S(2)}) async-start(f32[128,2,256]{2,1,0:T(2,128)} %bitcast.4), calls=%async_computation | async-start | bytes 524288 | tf_op jit(solution)/shard_map/all_to_all | solution.py:340
  14.5 0.7 constant_dynamic-slice_fusion
  15.2 4.2 %collective-permute-start = (f32[8,256]{1,0:T(8,128)S(1)}, f32[8,256]{1,0:T(8,128)S(1)}, u32[]{:S(2)}, u32[]{:S(2)}) collective-permute-start(f32[8,256]{1,0:T(8,128)S(1)} %constant_dynamic-slice_fusion), channel_id=1, source_target_pairs={{0,1},{1,0},{2,3},{3,2},{4,5},{5,4},{6,7},{7,6},{8,9},{9,8},{10,11... | collective-permute-start | bytes 24584 | tf_op jit(solution)/shard_map/ppermute | solution.py:353
  19.4 0.1 pad_add_fusion.where
  19.5 7.4 %all-to-all-done = f32[128,2,256]{2,1,0:T(2,128)S(1)} async-done(((f32[128,2,256]{2,1,0:T(2,128)}), f32[128,2,256]{2,1,0:T(2,128)S(1)}, u32[]{:S(2)}, u32[]{:S(2)}) %all-to-all-start) | async-done | bytes 262176 | tf_op jit(solution)/shard_map/all_to_all | solution.py:340
  26.9 0.2 reshape.17.coefs
  27.0 0.0 collective-permute-done.beside
  27.0 0.0 copy-start
  27.1 2.2 %copy-done = f32[4096,256]{1,0:T(8,128)S(1)} copy-done((f32[4096,256]{1,0:T(8,128)S(1)}, f32[4096,256]{1,0:T(8,128)}, u32[]{:S(2)}) %copy-start) | copy-done | bytes 4194328
  29.2 0.0 copy-start.4
  29.2 0.9 copy-done.4
  30.1 0.0 copy-start.7
  30.1 3.6 %expand.1 = f32[32,48,128]{2,1,0:T(8,128)} custom-call(s32[3]{0:T(128)S(1)} %pad_add_fusion.where, f32[256,256]{1,0:T(8,128)S(1)} %reshape.17.coefs, f32[128,256]{1,0:T(8,128)S(1)} %copy-done.4, f32[8,256]{1,0:T(8,128)S(1)} %collective-permute-done.beside, f32[4096,256]{1,0:T(8,128)S(1)} %copy-done), custom_call_target="tpu_custom_call" | custom-call | flops 1056964608 | bytes 3000000 | tf_op jit(solution)/shard_map/expand/pallas_call | solution.py:123
  33.8 0.0 copy-start.5
  33.8 4.1 %all-to-all-start.1 = ((f32[32,48,128]{2,1,0:T(8,128)}), f32[32,48,128]{2,1,0:T(8,128)S(1)}, u32[]{:S(2)}, u32[]{:S(2)}) async-start(f32[32,48,128]{2,1,0:T(8,128)} %expand.1), calls=%async_computation.1 | async-start | bytes 1572864 | tf_op jit(solution)/shard_map/all_to_all | solution.py:340
  37.9 0.0 copy-done.2
  37.9 0.0 copy-done.3
  38.0 0.4 collective-permute-start.1
  38.4 1.4 collective-permute-start.2
  39.8 10.9 %collective-permute-done.1.upper = f32[2,32,4,128]{3,2,1,0:T(4,128)S(1)} collective-permute-done((f32[2,32,4,128]{3,2,1,0:T(4,128)S(1)}, f32[2,32,4,128]{3,2,1,0:T(4,128)S(1)}, u32[]{:S(2)}, u32[]{:S(2)}) %collective-permute-start.1) | collective-permute-done | bytes 131104 | tf_op jit(solution)/shard_map/ppermute | solution.py:357
  50.7 0.0 collective-permute-done.2.lower
  50.7 3.4 %pack.1 = (f32[2,32,8,128]{3,2,1,0:T(8,128)S(1)}, f32[32,8,128]{2,1,0:T(8,128)S(1)}) custom-call(s32[3]{0:T(128)S(1)} %pad_add_fusion.where, f32[32,32,128]{2,1,0:T(8,128)S(1)} %copy-done.2, f32[32,32,128]{2,1,0:T(8,128)S(1)} %copy-done.3, f32[2,32,4,128]{3,2,1,0:T(4,128)S(1)} %collective-permute-done.1.upper, f32[2,32,4,128]{3,2,1,0:T(4,128)S(1)} %collective-permute-done.2.lower), custom_call_target="tpu_custom_call" | custom-call | flops 2000000 | bytes 1600000 | tf_op jit(solution)/shard_map/pack/pallas_call | solution.py:58
  54.1 4.6 %collective-permute-start.3 = (f32[32,8,128]{2,1,0:T(8,128)S(1)}, f32[32,8,128]{2,1,0:T(8,128)S(1)}, u32[]{:S(2)}, u32[]{:S(2)}) collective-permute-start(f32[32,8,128]{2,1,0:T(8,128)S(1)} %get-tuple-element.8), channel_id=1, source_target_pairs={{0,1},{1,0},{2,3},{3,2},{4,5},{5,4},{6,7},{7,6},{8,9},{9,8},{10,11... | collective-permute-start | bytes 393224 | tf_op jit(solution)/shard_map/ppermute | solution.py:360
  58.6 0.0 copy-done.7
  58.6 0.1 copy.7.basis_z
  58.7 6.6 %collective-permute-done.3.strip = f32[32,8,128]{2,1,0:T(8,128)S(1)} collective-permute-done((f32[32,8,128]{2,1,0:T(8,128)S(1)}, f32[32,8,128]{2,1,0:T(8,128)S(1)}, u32[]{:S(2)}, u32[]{:S(2)}) %collective-permute-start.3) | collective-permute-done | bytes 131104 | tf_op jit(solution)/shard_map/ppermute | solution.py:360
  65.3 0.0 all-to-all-done.1.layers
  65.3 34.7 %on_grid.1 = f32[32,32,128]{2,1,0:T(8,128)S(1)} custom-call(s32[3]{0:T(128)S(1)} %pad_add_fusion.where, f32[32,16]{1,0:T(8,128)S(1)} %copy.7.basis_z, f32[32,48,128]{2,1,0:T(8,128)S(1)} %all-to-all-done.1.layers, f32[32,32,128]{2,1,0:T(8,128)S(1)} %copy-done.2, f32[32,32,128]{2,1,0:T(8,128)S(1)} %copy-done.3, f32[2,32,8,128]{3,2,1,0:T(8,128)S(1)} %get-tuple-element.7.rows, ...), custom_call_target="tpu_custom_call" | custom-call | flops 100000000 | bytes 3000000 | tf_op jit(solution)/shard_map/on_grid/pallas_call | solution.py:274
  100.0 0.0 copy-start.6
  100.0 18.5 %all_to_all.25 = f32[32,32,128]{2,1,0:T(8,128)S(1)} all-to-all(f32[32,32,128]{2,1,0:T(8,128)S(1)} %on_grid.1), channel_id=1, replica_groups=mesh['y'=4,'zl'=4,'x'=4,'core'=2,'zh'=2] {'y','x','core'}, dimensions={0} | all-to-all | bytes 1048576 | tf_op jit(solution)/shard_map/all_to_all | solution.py:340
  118.5 0.0 copy-done.5
  118.5 0.0 copy-start.1
  118.5 2.2 %copy-done.1 = f32[4096,256]{1,0:T(8,128)S(1)} copy-done((f32[4096,256]{1,0:T(8,128)S(1)}, f32[4096,256]{1,0:T(8,128)}, u32[]{:S(2)}) %copy-start.1) | copy-done | bytes 4194328
  120.7 2.3 %project.1 = f32[8,64,128]{2,1,0:T(8,128)S(1)} custom-call(s32[3]{0:T(128)S(1)} %pad_add_fusion.where, f32[1024,128]{1,0:T(8,128)S(1)} %bitcast.12, f32[128,256]{1,0:T(8,128)S(1)} %copy-done.5, f32[4096,256]{1,0:T(8,128)S(1)} %copy-done.1), custom_call_target="tpu_custom_call" | custom-call | flops 503316480 | bytes 2000000 | tf_op jit(solution)/shard_map/project/pallas_call | solution.py:322
  123.1 17.2 %all_to_all.26 = f32[8,64,128]{2,1,0:T(8,128)S(1)} all-to-all(f32[8,64,128]{2,1,0:T(8,128)S(1)} %project.1), channel_id=1, replica_groups=mesh['y'=4,'zl'=4,'x'=4,'core'=2,'zh'=2] {'zl','zh'}, dimensions={0} | all-to-all | bytes 524288 | tf_op jit(solution)/shard_map/all_to_all | solution.py:340
  140.2 0.6 reduce_sum.9
  140.9 4.0 %all-to-all-start.4 = ((f32[32,2,128]{2,1,0:T(2,128)}), f32[32,2,128]{2,1,0:T(2,128)S(1)}, u32[]{:S(2)}, u32[]{:S(2)}) async-start(f32[32,2,128]{2,1,0:T(2,128)} %bitcast.8), calls=%async_computation.4 | async-start | bytes 65536 | tf_op jit(solution)/shard_map/all_to_all | solution.py:340
  144.9 7.4 %all-to-all-done.4 = f32[32,2,128]{2,1,0:T(2,128)S(1)} async-done(((f32[32,2,128]{2,1,0:T(2,128)}), f32[32,2,128]{2,1,0:T(2,128)S(1)}, u32[]{:S(2)}, u32[]{:S(2)}) %all-to-all-start.4) | async-done | bytes 32800 | tf_op jit(solution)/shard_map/all_to_all | solution.py:340
  152.2 0.0 copy-done.6
  152.2 0.6 dynamic-slice_add_fusion
  (1 shorter events, 0.0 us)
Async XLA Ops:
  0.0 37.9 %copy-start.2 = (f32[32,32,128]{2,1,0:T(8,128)S(1)}, f32[32,32,128]{2,1,0:T(8,128)}, u32[]{:S(2)}) copy-start(f32[32,32,128]{2,1,0:T(8,128)} %kap.3) | copy-start | bytes 1572868
  0.0 37.9 %copy-start.3 = (f32[32,32,128]{2,1,0:T(8,128)S(1)}, f32[32,32,128]{2,1,0:T(8,128)}, u32[]{:S(2)}) copy-start(f32[32,32,128]{2,1,0:T(8,128)} %prs.3) | copy-start | bytes 1572868
  1.7 25.1 %all-to-all-start = ((f32[128,2,256]{2,1,0:T(2,128)}), f32[128,2,256]{2,1,0:T(2,128)S(1)}, u32[]{:S(2)}, u32[]{:S(2)}) async-start(f32[128,2,256]{2,1,0:T(2,128)} %bitcast.4), calls=%async_computation | async-start | bytes 524288 | tf_op jit(solution)/shard_map/all_to_all | solution.py:340
  15.2 11.8 %collective-permute-start = (f32[8,256]{1,0:T(8,128)S(1)}, f32[8,256]{1,0:T(8,128)S(1)}, u32[]{:S(2)}, u32[]{:S(2)}) collective-permute-start(f32[8,256]{1,0:T(8,128)S(1)} %constant_dynamic-slice_fusion), channel_id=1, source_target_pairs={{0,1},{1,0},{2,3},{3,2},{4,5},{5,4},{6,7},{7,6},{8,9},{9,8},{10,11... | collective-permute-start | bytes 24584 | tf_op jit(solution)/shard_map/ppermute | solution.py:353
  27.0 2.2 %copy-start = (f32[4096,256]{1,0:T(8,128)S(1)}, f32[4096,256]{1,0:T(8,128)}, u32[]{:S(2)}) copy-start(f32[4096,256]{1,0:T(8,128)} %first_basis.3) | copy-start | bytes 12582916
  29.2 0.9 copy-start.4
  30.1 28.5 %copy-start.7 = (f32[32,16]{0,1:T(8,128)S(1)}, f32[32,16]{0,1:T(8,128)}, u32[]{:S(2)}) copy-start(f32[32,16]{0,1:T(8,128)} %param.9) | copy-start | bytes 6148
  33.8 84.8 %copy-start.5 = (f32[128,256]{1,0:T(8,128)S(1)}, f32[128,256]{1,0:T(8,128)}, u32[]{:S(2)}) copy-start(f32[128,256]{1,0:T(8,128)} %basis.3) | copy-start | bytes 393220
  33.8 31.5 %all-to-all-start.1 = ((f32[32,48,128]{2,1,0:T(8,128)}), f32[32,48,128]{2,1,0:T(8,128)S(1)}, u32[]{:S(2)}, u32[]{:S(2)}) async-start(f32[32,48,128]{2,1,0:T(8,128)} %expand.1), calls=%async_computation.1 | async-start | bytes 1572864 | tf_op jit(solution)/shard_map/all_to_all | solution.py:340
  38.0 12.7 %collective-permute-start.1 = (f32[2,32,4,128]{3,2,1,0:T(4,128)S(1)}, f32[2,32,4,128]{3,2,1,0:T(4,128)S(1)}, u32[]{:S(2)}, u32[]{:S(2)}) collective-permute-start(f32[2,32,4,128]{3,2,1,0:T(4,128)S(1)} %get-tuple-element.10), channel_id=1, source_target_pairs={{2,0},{4,2},{6,4},{8,6},{10,8},{12,10},{14,12},{16,14},{18,16},{20... | collective-permute-start | bytes 393224 | tf_op jit(solution)/shard_map/ppermute | solution.py:357
  38.4 12.3 %collective-permute-start.2 = (f32[2,32,4,128]{3,2,1,0:T(4,128)S(1)}, f32[2,32,4,128]{3,2,1,0:T(4,128)S(1)}, u32[]{:S(2)}, u32[]{:S(2)}) collective-permute-start(f32[2,32,4,128]{3,2,1,0:T(4,128)S(1)} %get-tuple-element.9), channel_id=1, source_target_pairs={{0,2},{2,4},{4,6},{6,8},{8,10},{10,12},{12,14},{14,16},{16,18},{18... | collective-permute-start | bytes 393224 | tf_op jit(solution)/shard_map/ppermute | solution.py:358
  54.1 11.2 %collective-permute-start.3 = (f32[32,8,128]{2,1,0:T(8,128)S(1)}, f32[32,8,128]{2,1,0:T(8,128)S(1)}, u32[]{:S(2)}, u32[]{:S(2)}) collective-permute-start(f32[32,8,128]{2,1,0:T(8,128)S(1)} %get-tuple-element.8), channel_id=1, source_target_pairs={{0,1},{1,0},{2,3},{3,2},{4,5},{5,4},{6,7},{7,6},{8,9},{9,8},{10,11... | collective-permute-start | bytes 393224 | tf_op jit(solution)/shard_map/ppermute | solution.py:360
  100.0 52.3 %copy-start.6 = (f32[2,16,2,256]{3,2,1,0:T(2,128)S(1)}, f32[2,16,2,256]{3,2,1,0:T(2,128)}, u32[]{:S(2)}) copy-start(f32[2,16,2,256]{3,2,1,0:T(2,128)} %param.6) | copy-start | bytes 196612
  118.5 2.2 %copy-start.1 = (f32[4096,256]{1,0:T(8,128)S(1)}, f32[4096,256]{1,0:T(8,128)}, u32[]{:S(2)}) copy-start(f32[4096,256]{1,0:T(8,128)} %first_basis.3) | copy-start | bytes 12582916
  140.9 11.4 %all-to-all-start.4 = ((f32[32,2,128]{2,1,0:T(2,128)}), f32[32,2,128]{2,1,0:T(2,128)S(1)}, u32[]{:S(2)}, u32[]{:S(2)}) async-start(f32[32,2,128]{2,1,0:T(2,128)} %bitcast.8), calls=%async_computation.4 | async-start | bytes 65536 | tf_op jit(solution)/shard_map/all_to_all | solution.py:340
where the time goes:
time: 153 us
  Pallas kernels  44 us (29%)
  blocking collectives  35.7 us (23%)
  waiting for transfers between devices  32.2 us (21%)
  starting transfers between devices  31.5 us (21%)
  local copies, waits for them, and re-layouts  7.98 us (5%)
    all_to_all x2, blocking collectives, exchanged(): return lax.all_to_all(values, axes, split_axis=0, concat_axis=0, tiled=True)  35.7 us
    pallas_call x1, Pallas kernels, on_grid(): pl.pallas_call(grid_kernel, out_shape=jax.ShapeDtypeStruct((DIRECTIONS *...  34.7 us
    all_to_all x3, starting transfers between devices, exchanged(): return lax.all_to_all(values, axes, split_axis=0, concat_axis=0, tiled=True)  20.9 us
    all_to_all x3, waiting for transfers between devices, exchanged(): return lax.all_to_all(values, axes, split_axis=0, concat_axis=0, tiled=True)  14.7 us
    ppermute x1, waiting for transfers between devices, per_device(): lax.ppermute(statics[:, :, :HALO], GX, [((i + 1) % 128, i) for i in range...  10.9 us
    ppermute x1, waiting for transfers between devices, per_device(): strip = lax.ppermute(strip, 'zh', swap)  6.59 us
    unnamed x17, local copies, waits for them, and re-layouts  5.37 us
    ppermute x1, starting transfers between devices, per_device(): strip = lax.ppermute(strip, 'zh', swap)  4.56 us
  transfers between devices with their start and end apart: 7, of which 4 were waited for; matrix products, arithmetic and copies ran while one was open for 1% of the time, Pallas kernels for 2%

commit v1 on v0

v1 whole, which is shorter than its diff:
```python
import jax
import jax.numpy as jnp
from jax import lax
from jax.experimental import pallas as pl
from jax.experimental.pallas import tpu as pltpu
from jax.sharding import Mesh, PartitionSpec as P

step_size = 0.05
highest = lax.Precision.HIGHEST
f32 = jnp.float32

AXES = ("y", "zl", "x", "core", "zh")
SIZES = (4, 4, 4, 2, 2)
GX = ("y", "zl", "x", "core")
PLANE = ("y", "x", "core")
RING = ("zl", "zh")

DIRECTIONS, MODES_Z, DEPTH = 2, 16, 32
ROWS, COLS = 32, 128
HALO = 4
EXT_ROWS = ROWS + 2 * HALO
EXT_COLS = 2 * COLS
STRIP = 8
GROUPS = EXT_ROWS // STRIP
PER_STEP = 16
LAYER_STEP = 4
STATIC_STEP = 8
MODES = 256
FIELDS = 14
BLOCK = 8 * ROWS
VMEM = pl.BlockSpec(memory_space=pltpu.VMEM)
SMEM = pl.BlockSpec(memory_space=pltpu.SMEM)
HBM = pl.BlockSpec(memory_space=pltpu.HBM)


def params(mib):
    return pltpu.CompilerParams(vmem_limit_bytes=mib * 1024 * 1024)


def strip_shift(zh, lane):
    return lax.rem(120 * zh + 2 * COLS - lane, COLS)


def columns_on(c, h, last):
    c, h = pltpu.roll(c, COLS - 1, 1), pltpu.roll(h, COLS - 1, 1)
    return jnp.where(last, h, c), jnp.where(last, c, h)


def pack_kernel(where, kap, prs, upper, lower, rows_out, strip_out):
    zh = where[1]
    lane = lax.broadcasted_iota(jnp.int32, (STRIP, COLS), 1)

    def body(i, carry):
        for j in range(LAYER_STEP):
            z = i * LAYER_STEP + j
            packed = jnp.zeros((STRIP, COLS), f32)
            for f, ref in enumerate((kap, prs)):
                beside = jnp.concatenate([upper[f, z], lower[f, z]], axis=0)
                rows_out[f, z] = beside
                for g in range(GROUPS):
                    tile = ref[z, pl.ds(8 * g, 8)] if g < ROWS // 8 else beside
                    first = f * EXT_ROWS + 8 * g
                    moved = pltpu.roll(tile, lax.rem(first + 8 * (1 - zh), COLS), 1)
                    packed = jnp.where((lane >= first) & (lane < first + 8), moved, packed)
            strip_out[z] = packed
        return carry

    lax.fori_loop(0, DEPTH // LAYER_STEP, body, 0)


def pack(where, kap, prs, upper, lower):
    return pl.pallas_call(
        pack_kernel,
        out_shape=(
            jax.ShapeDtypeStruct((2, DEPTH, 2 * HALO, COLS), f32),
            jax.ShapeDtypeStruct((DEPTH, STRIP, COLS), f32),
        ),
        in_specs=[SMEM] + [VMEM] * 4,
        out_specs=(VMEM, VMEM),
        compiler_params=params(52),
        cost_estimate=pl.CostEstimate(flops=2_000_000, bytes_accessed=1_600_000, transcendentals=0),
        name="pack",
    )(where, kap, prs, upper, lower)


def expand_kernel(where, coefs, basis, beside, first_basis, out, wide, blocks, sems):
    zl = where[2]
    copies = []
    for y in range(4):
        start = pl.multiple_of((y * 4 + zl) * BLOCK, BLOCK)
        below = pl.multiple_of(jnp.maximum(start - 8, 0), 8)
        above = pl.multiple_of(jnp.minimum(start + BLOCK, 4096 - 8), 8)
        for part, (src, size, dst) in enumerate(
            ((below, 8, 0), (start, BLOCK, 8), (above, 8, BLOCK + 8))
        ):
            copies.append(
                pltpu.make_async_copy(
                    first_basis.at[pl.ds(src, size)],
                    blocks.at[y, pl.ds(dst, size)],
                    sems.at[y, part],
                )
            )
    for copy in copies:
        copy.start()
    wide[pl.ds(0, COLS)] = basis[...]
    wide[pl.ds(COLS, STRIP)] = beside[...]
    wide[pl.ds(COLS + STRIP, COLS - STRIP)] = jnp.zeros((COLS - STRIP, MODES), f32)
    columns = lax.dot_general(
        coefs[...], wide[...], (((1,), (1,)), ((), ())),
        precision=highest, preferred_element_type=f32,
    )
    lane = lax.broadcasted_iota(jnp.int32, (STRIP, COLS), 1)
    low = lax.broadcasted_iota(jnp.int32, (STRIP, EXT_COLS), 0) < HALO
    for copy in copies:
        copy.wait()
    for y in range(4):
        full = lax.dot_general(
            blocks[y], columns, (((1,), (0,)), ((), ())),
            precision=highest, preferred_element_type=f32,
        )
        for k in range(8):
            own = full[8 + ROWS * k : 8 + ROWS * (k + 1)]
            above = full[8 + ROWS * (k + 1) : 16 + ROWS * (k + 1)]
            below = full[ROWS * k : ROWS * k + 8]
            ends = jnp.where(low, above, below)
            q = y * 8 + k
            out[q, pl.ds(0, ROWS)] = own[:, :COLS]
            out[q, pl.ds(ROWS, 8)] = ends[:, :COLS]
            packed = own[:8, COLS:]
            for g in range(1, GROUPS):
                tile = (own[8 * g : 8 * g + 8] if g < ROWS // 8 else ends)[:, COLS:]
                packed = jnp.where(lane < 8 * g, packed, pltpu.roll(tile, 8 * g, 1))
            out[q, pl.ds(EXT_ROWS, STRIP)] = packed


def expand(where, coefs, basis, beside, first_basis):
    return pl.pallas_call(
        expand_kernel,
        out_shape=jax.ShapeDtypeStruct((32, EXT_ROWS + STRIP, COLS), f32),
        in_specs=[SMEM, VMEM, VMEM, VMEM, HBM],
        out_specs=VMEM,
        scratch_shapes=[
            pltpu.VMEM((EXT_COLS, MODES), f32),
            pltpu.VMEM((4, BLOCK + 16, MODES), f32),
            pltpu.SemaphoreType.DMA((4, 3)),
        ],
        compiler_params=params(52),
        cost_estimate=pl.CostEstimate(
            flops=6 * 2 * 256 * 256 * 1344, bytes_accessed=3_000_000, transcendentals=0
        ),
        name="expand",
    )(where, coefs, basis, beside, first_basis)


def statics_kernel(where, kap, prs, rows, strip, out, built, pp, ph, sem):
    kk, kh, pxc, pxh, pyc, pyh, pzc, pzh, exc, exh, eyc, eyh, ezc, ezh = (
        built.at[n] for n in range(FIELDS)
    )
    gx, zh = where[0], where[1]
    half = 0.5 * step_size * step_size

    def place(i, carry):
        for j in range(STATIC_STEP):
            z = i * STATIC_STEP + j
            packed = strip[z]
            for f, (src, dst, far) in enumerate(((kap, kk, kh), (prs, pp, ph))):
                ends = rows[f, z]
                dst[z, pl.ds(HALO, ROWS)] = src[z]
                dst[z, pl.ds(0, HALO)] = ends[HALO:]
                dst[z, pl.ds(HALO + ROWS, HALO)] = ends[:HALO]
                for g in range(GROUPS):
                    tile = pltpu.roll(packed, strip_shift(zh, f * EXT_ROWS + 8 * g), 1)
                    if g < ROWS // 8:
                        far[z, pl.ds(HALO + 8 * g, 8)] = tile
                    else:
                        far[z, pl.ds(0, HALO)] = tile[HALO:]
                        far[z, pl.ds(HALO + ROWS, HALO)] = tile[:HALO]
        return carry

    lax.fori_loop(0, DEPTH // STATIC_STEP, place, 0)

    lane = lax.broadcasted_iota(jnp.int32, (8, COLS), 1)
    row = lax.broadcasted_iota(jnp.int32, (8, COLS), 0)
    last = lane == COLS - 1
    mask_c = jnp.where(last & (zh == 1), 0.0, 1.0).astype(f32)
    mask_h = jnp.where(last & (zh == 0), 0.0, 1.0).astype(f32)
    lowest, highest_row = jnp.where(gx == 0, HALO - 1, -1), jnp.where(gx == 127, HALO + ROWS - 1, -1)

    for start in (0, 8, 16, 24, 31):
        at, up = pl.ds(start, 8), pl.ds(start + 1, 8)
        here = row + start
        mask_x = jnp.where((here == lowest) | (here == highest_row), 0.0, 1.0).astype(f32)

        def along_x(i, carry, at=at, up=up, mask_x=mask_x):
            for j in range(STATIC_STEP):
                z = i * STATIC_STEP + j
                exc[z, at] = (half * mask_x) * (kk[z, at] + kk[z, up])
                exh[z, at] = (half * mask_x) * (kh[z, at] + kh[z, up])
                pxc[z, at] = (0.5 * mask_x) * (pp[z, up] - pp[z, at])
                pxh[z, at] = (0.5 * mask_x) * (ph[z, up] - ph[z, at])
            return carry

        lax.fori_loop(0, DEPTH // STATIC_STEP, along_x, 0)

    for start in (0, 8, 16, 24, 32):
        at = pl.ds(start, 8)

        def along_yz(i, carry, at=at):
            for j in range(STATIC_STEP):
                z = i * STATIC_STEP + j
                later = jnp.minimum(z + 1, DEPTH - 1)
                inside = jnp.where(z < DEPTH - 1, 1.0, 0.0).astype(f32)
                c, h, p, q = kk[z, at], kh[z, at], pp[z, at], ph[z, at]
                cn, hn = columns_on(c, h, last)
                pn, qn = columns_on(p, q, last)
                eyc[z, at] = (half * mask_c) * (c + cn)
                eyh[z, at] = (half * mask_h) * (h + hn)
                pyc[z, at] = (0.5 * mask_c) * (pn - p)
                pyh[z, at] = (0.5 * mask_h) * (qn - q)
                ezc[z, at] = (half * inside) * (c + kk[later, at])
                ezh[z, at] = (half * inside) * (h + kh[later, at])
                pzc[z, at] = (0.5 * inside) * (pp[later, at] - p)
                pzh[z, at] = (0.5 * inside) * (ph[later, at] - q)
            return carry

        lax.fori_loop(0, DEPTH // STATIC_STEP, along_yz, 0)

    copy = pltpu.make_async_copy(built, out, sem)
    copy.start()
    copy.wait()


def statics(where, kap, prs, rows, strip):
    field = (DEPTH, EXT_ROWS, COLS)
    return pl.pallas_call(
        statics_kernel,
        out_shape=jax.ShapeDtypeStruct((FIELDS,) + field, f32),
        in_specs=[SMEM] + [VMEM] * 4,
        out_specs=HBM,
        scratch_shapes=[
            pltpu.VMEM((FIELDS,) + field, f32),
            pltpu.VMEM(field, f32),
            pltpu.VMEM(field, f32),
            pltpu.SemaphoreType.DMA,
        ],
        compiler_params=params(52),
        cost_estimate=pl.CostEstimate(
            flops=20_000_000, bytes_accessed=12_000_000, transcendentals=0
        ),
        name="statics",
    )(where, kap, prs, rows, strip)


def grid_kernel(where, basis_z, layers, kap, fields, out, built, uc, uh, vc, vh, sens, sems):
    kk, kh, pxc, pxh, pyc, pyh, pzc, pzh, exc, exh, eyc, eyh, ezc, ezh = (
        built.at[n] for n in range(FIELDS)
    )
    copies = [
        pltpu.make_async_copy(
            fields.at[pl.ds(first, size)], built.at[pl.ds(first, size)], sems.at[n]
        )
        for n, (first, size) in enumerate(((0, 2), (2, 6), (8, 6)))
    ]
    for copy in copies:
        copy.start()
    copies[0].wait()
    zh = where[1]
    lane = lax.broadcasted_iota(jnp.int32, (8, COLS), 1)
    first, last = lane == 0, lane == COLS - 1
    tiles = (EXT_ROWS + STRIP) // 8

    def layers_of(i, carry):
        for d in range(DIRECTIONS):
            totals = [[None] * tiles for _ in range(LAYER_STEP)]
            for c in range(MODES_Z):
                parts = [layers[d * MODES_Z + c, pl.ds(8 * t, 8)] for t in range(tiles)]
                for j in range(LAYER_STEP):
                    weight = basis_z[i * LAYER_STEP + j, c]
                    for t in range(tiles):
                        term = weight * parts[t]
                        totals[j][t] = term if c == 0 else totals[j][t] + term
            for j in range(LAYER_STEP):
                z = i * LAYER_STEP + j
                packed = totals[j][tiles - 1]
                for g in range(GROUPS):
                    tile = pltpu.roll(packed, strip_shift(zh, 8 * g), 1)
                    if g < ROWS // 8:
                        at = pl.ds(HALO + 8 * g, 8)
                        uc[d, z, at] = kk[z, at] * totals[j][g]
                        uh[d, z, at] = kh[z, at] * tile
                    else:
                        low, high = pl.ds(0, HALO), pl.ds(HALO + ROWS, HALO)
                        uc[d, z, low] = kk[z, low] * totals[j][g][HALO:]
                        uh[d, z, low] = kh[z, low] * tile[HALO:]
                        uc[d, z, high] = kk[z, high] * totals[j][g][:HALO]
                        uh[d, z, high] = kh[z, high] * tile[:HALO]
        return carry

    lax.fori_loop(0, DEPTH // LAYER_STEP, layers_of, 0)

    def columns_back(c, h):
        c, h = pltpu.roll(c, 1, 1), pltpu.roll(h, 1, 1)
        return jnp.where(first, h, c), jnp.where(first, c, h)

    zero = jnp.zeros((8, COLS), f32)

    def sweep(starts, source, target, coeffs, join, scale):
        (src_c, src_h), (dst_c, dst_h) = source, target
        (axc, axh), (ayc, ayh), (azc, azh) = coeffs
        for start in starts:
            at, up, down = pl.ds(start, 8), pl.ds(start + 1, 8), pl.ds(start - 1, 8)

            def body(i, carry, at=at, up=up, down=down):
                carry = list(carry)
                for j in range(PER_STEP):
                    z = i * PER_STEP + j
                    later = jnp.minimum(z + 1, DEPTH - 1)
                    for d in range(DIRECTIONS):
                        c, h, fzc, fzh = carry[4 * d : 4 * d + 4]
                        cz, hz = src_c[d, later, at], src_h[d, later, at]
                        cy, hy = columns_on(c, h, last)
                        fyc, fyh = join(cy, c) * ayc[z, at], join(hy, h) * ayh[z, at]
                        byc, byh = columns_back(fyc, fyh)
                        gzc, gzh = join(cz, c) * azc[z, at], join(hz, h) * azh[z, at]
                        xc = (
                            join(src_c[d, z, up], c) * axc[z, at]
                            - join(c, src_c[d, z, down]) * axc[z, down]
                        )
                        xh = (
                            join(src_h[d, z, up], h) * axh[z, at]
                            - join(h, src_h[d, z, down]) * axh[z, down]
                        )
                        total_c = xc + (fyc - byc) + (gzc - fzc)
                        total_h = xh + (fyh - byh) + (gzh - fzh)
                        if scale is not None:
                            total_c = scale * c + total_c
                            total_h = scale * h + total_h
                        dst_c[d, z, at] = total_c
                        dst_h[d, z, at] = total_h
                        carry[4 * d : 4 * d + 4] = [cz, hz, gzc, gzh]
                return tuple(carry)

            begin = []
            for d in range(DIRECTIONS):
                begin += [src_c[d, 0, at], src_h[d, 0, at], zero, zero]
            lax.fori_loop(0, DEPTH // PER_STEP, body, tuple(begin))

    def plus(a, b):
        return a + b

    def minus(a, b):
        return a - b

    u, v = (uc, uh), (vc, vh)
    ps = ((pxc, pxh), (pyc, pyh), (pzc, pzh))
    es = ((exc, exh), (eyc, eyh), (ezc, ezh))
    copies[1].wait()
    sweep((1, 9, 17, 25, 31), u, v, ps, plus, None)
    copies[2].wait()
    sweep((2, 10, 18, 26, 30), v, u, es, minus, 2.0 * step_size)
    sweep((3, 11, 19, 27, 29), u, v, es, minus, 2.0 * step_size)

    for start in (4, 12, 20, 28):
        at, up, down = pl.ds(start, 8), pl.ds(start + 1, 8), pl.ds(start - 1, 8)
        own = pl.ds(start - HALO, 8)

        def couple(i, carry, at=at, up=up, down=down, own=own):
            carry = list(carry)
            for j in range(PER_STEP):
                z = i * PER_STEP + j
                later = jnp.minimum(z + 1, DEPTH - 1)
                for d in range(DIRECTIONS):
                    c, fzc = carry[2 * d : 2 * d + 2]
                    h = vh[d, z, at]
                    cz = vc[d, later, at]
                    cy, hy = columns_on(c, h, last)
                    fyc, fyh = (cy - c) * pyc[z, at], (hy - h) * pyh[z, at]
                    byc, _ = columns_back(fyc, fyh)
                    gzc = (cz - c) * pzc[z, at]
                    xc = (vc[d, z, up] - c) * pxc[z, at] + (c - vc[d, z, down]) * pxc[z, down]
                    sens[d, z, own] = -kap[z, own] * (xc + (fyc + byc) + (gzc + fzc))
                    carry[2 * d : 2 * d + 2] = [cz, gzc]
            return tuple(carry)

        begin = []
        for d in range(DIRECTIONS):
            begin += [vc[d, 0, at], zero]
        lax.fori_loop(0, DEPTH // PER_STEP, couple, tuple(begin))

    def modes_of(c, carry):
        for d in range(DIRECTIONS):
            total = basis_z[0, c] * sens[d, 0]
            for z in range(1, DEPTH):
                total = total + basis_z[z, c] * sens[d, z]
            out[d * MODES_Z + c] = total
        return carry

    lax.fori_loop(0, MODES_Z, modes_of, 0)


def on_grid(where, basis_z, layers, kap, fields):
    wide = (DIRECTIONS, DEPTH, EXT_ROWS, COLS)
    return pl.pallas_call(
        grid_kernel,
        out_shape=jax.ShapeDtypeStruct((DIRECTIONS * MODES_Z, ROWS, COLS), f32),
        in_specs=[SMEM, SMEM, VMEM, VMEM, HBM],
        out_specs=VMEM,
        scratch_shapes=[pltpu.VMEM((FIELDS, DEPTH, EXT_ROWS, COLS), f32)]
        + [pltpu.VMEM(wide, f32) for _ in range(4)]
        + [
            pltpu.VMEM((DIRECTIONS, DEPTH, ROWS, COLS), f32),
            pltpu.SemaphoreType.DMA((3,)),
        ],
        compiler_params=params(52),
        cost_estimate=pl.CostEstimate(
            flops=100_000_000, bytes_accessed=12_000_000, transcendentals=0
        ),
        name="on_grid",
    )(where, basis_z, layers, kap, fields)


def project_kernel(where, values, basis, first_basis, out, blocks, sems):
    zl = where[2]
    copies = []
    for y in range(4):
        start = pl.multiple_of((y * 4 + zl) * BLOCK, BLOCK)
        copies.append(
            pltpu.make_async_copy(
                first_basis.at[pl.ds(start, BLOCK)], blocks.at[pl.ds(y * BLOCK, BLOCK)], sems.at[y]
            )
        )
    for copy in copies:
        copy.start()
    for copy in copies:
        copy.wait()
    along_x = lax.dot_general(
        blocks[...], values[...], (((0,), (0,)), ((), ())),
        precision=highest, preferred_element_type=f32,
    )
    full = lax.dot_general(
        along_x, basis[...], (((1,), (0,)), ((), ())),
        precision=highest, preferred_element_type=f32,
    )
    for y in range(4):
        for z in range(4):
            at = y * 64 + z * 16
            for h in range(2):
                out[z * 2 + h, pl.ds(y * 16, 16)] = full[at : at + 16, h * 128 : (h + 1) * 128]


def project(where, values, basis, first_basis):
    return pl.pallas_call(
        project_kernel,
        out_shape=jax.ShapeDtypeStruct((8, 64, 128), f32),
        in_specs=[SMEM, VMEM, VMEM, HBM],
        out_specs=VMEM,
        scratch_shapes=[
            pltpu.VMEM((4 * BLOCK, MODES), f32),
            pltpu.SemaphoreType.DMA((4,)),
        ],
        compiler_params=params(52),
        cost_estimate=pl.CostEstimate(
            flops=6 * 2 * 256 * 128 * 1280, bytes_accessed=2_000_000, transcendentals=0
        ),
        name="project",
    )(where, values, basis, first_basis)


def exchanged(values, axes):
    return lax.all_to_all(values, axes, split_axis=0, concat_axis=0, tiled=True)


def per_device(coefficients, first_axis_basis, basis_y, basis_z, conductivity, pressure):
    gx = lax.axis_index(GX)
    zh = lax.axis_index("zh")
    where = jnp.stack([gx, zh, lax.axis_index("zl")]).astype(jnp.int32)
    swap = [(0, 1), (1, 0)]

    flat = coefficients.reshape(DIRECTIONS * MODES_Z, 2, MODES)
    spread = jnp.broadcast_to(flat.reshape(4, 1, 8, 2, MODES), (4, 4, 8, 2, MODES))
    gathered = exchanged(spread.reshape(128, 2, MODES), GX)

    beside = lax.ppermute(
        lax.dynamic_slice_in_dim(basis_y, (COLS - STRIP) * (1 - zh), STRIP, 0), "zh", swap
    )
    both = jnp.stack([conductivity, pressure])
    upper = lax.ppermute(both[:, :, :HALO], GX, [((i + 1) % 128, i) for i in range(128)])
    lower = lax.ppermute(both[:, :, -HALO:], GX, [(i, (i + 1) % 128) for i in range(128)])
    rows, strip = pack(where, conductivity, pressure, upper, lower)
    gathered, rows = lax.optimization_barrier((gathered, rows))
    strip = lax.ppermute(strip, "zh", swap)

    message = expand(where, gathered.reshape(MODES, MODES), basis_y, beside, first_axis_basis)
    fields = statics(where, conductivity, pressure, rows, strip)
    layers = exchanged(message, PLANE)
    modes = on_grid(where, basis_z, layers, conductivity, fields)
    columns = exchanged(modes, PLANE)
    shares = project(where, columns.reshape(4 * BLOCK, COLS), basis_y, first_axis_basis)
    summed = jnp.sum(exchanged(shares, RING), axis=0)
    result = exchanged(summed.reshape(32, 2, 128), PLANE)
    own = lax.dynamic_slice_in_dim(coefficients, zh * 128, 128, 3)
    return result.reshape(DIRECTIONS, MODES_Z, 2, 128) + own


def solution(mesh):
    split = Mesh(mesh.devices.reshape(SIZES), AXES)
    return jax.shard_map(
        per_device,
        mesh=split,
        in_specs=(
            P(None, None, GX, None),
            P(),
            P("zh", None),
            P(),
            P(None, GX, "zh"),
            P(None, GX, "zh"),
        ),
        out_specs=P(None, None, GX, "zh"),
        check_vma=False,
    )
```

time: 153 us -> 130 us (0.85)
  waiting for transfers between devices: 32.2 us -> 13.8 us
  Pallas kernels: 44 us -> 34.4 us
  blocking collectives: 35.7 us -> 39.5 us
  local copies, waits for them, and re-layouts: 7.98 us -> 5.69 us
  starting transfers between devices: 31.5 us -> 33.7 us
    pallas_call x1, Pallas kernels: 34.7 us -> 17.4 us  [on_grid(): pl.pallas_call(grid_kernel, out_shape=jax.ShapeDtypeStruct((DIRECTIONS *...]
    ppermute x2, waiting for transfers between devices: 10.9 us -> 0.33 us  [the longest x1 0.33 us: per_device(): lax.ppermute(both[:, :, :HALO], GX, [((i + 1) % 128, i) for i in range(12...]
    pallas_call x0 -> x1, Pallas kernels: none -> 7.97 us  [statics(): pl.pallas_call(statics_kernel, out_shape=jax.ShapeDtypeStruct((FIELDS,) +...]
    all_to_all x3, waiting for transfers between devices: 14.7 us -> 8.94 us  [exchanged(): return lax.all_to_all(values, axes, split_axis=0, concat_axis=0, tiled=True)]
    all_to_all x2, blocking collectives: 35.7 us -> 39.5 us  [exchanged(): return lax.all_to_all(values, axes, split_axis=0, concat_axis=0, tiled=True)]
    all_to_all x3, starting transfers between devices: 20.9 us -> 23.5 us  [exchanged(): return lax.all_to_all(values, axes, split_axis=0, concat_axis=0, tiled=True)]
    unnamed x17, local copies, waits for them, and re-layouts: 5.37 us -> 3.08 us
    ppermute x1, waiting for transfers between devices: 6.59 us -> 4.48 us  [per_device(): strip = lax.ppermute(strip, 'zh', swap)]
  transfers between devices with their start and end apart: 7 -> 7, of which waited for: 4 -> 4; matrix products, arithmetic and copies ran while one was open for 1% -> 2% of each run, Pallas kernels for 2% -> 7%
where the time goes in v1:
time: 130 us
  blocking collectives  39.5 us (30%)
  Pallas kernels  34.4 us (26%)
  starting transfers between devices  33.7 us (26%)
  waiting for transfers between devices  13.8 us (11%)
  local copies, waits for them, and re-layouts  5.69 us (4%)
  other arithmetic  2.49 us (2%)
    all_to_all x2, blocking collectives, exchanged(): return lax.all_to_all(values, axes, split_axis=0, concat_axis=0, tiled=True)  39.5 us
    all_to_all x3, starting transfers between devices, exchanged(): return lax.all_to_all(values, axes, split_axis=0, concat_axis=0, tiled=True)  23.5 us
    pallas_call x1, Pallas kernels, on_grid(): pl.pallas_call(grid_kernel, out_shape=jax.ShapeDtypeStruct((DIRECTIONS *...  17.4 us
    all_to_all x3, waiting for transfers between devices, exchanged(): return lax.all_to_all(values, axes, split_axis=0, concat_axis=0, tiled=True)  8.94 us
    pallas_call x1, Pallas kernels, statics(): pl.pallas_call(statics_kernel, out_shape=jax.ShapeDtypeStruct((FIELDS,) +...  7.97 us
    ppermute x1, waiting for transfers between devices, per_device(): strip = lax.ppermute(strip, 'zh', swap)  4.48 us
    ppermute x1, starting transfers between devices, per_device(): strip = lax.ppermute(strip, 'zh', swap)  4.48 us
    pallas_call x1, Pallas kernels, expand(): pl.pallas_call(expand_kernel, out_shape=jax.ShapeDtypeStruct((32, EXT_ROW...  4.23 us
  transfers between devices with their start and end apart: 7, of which 4 were waited for; matrix products, arithmetic and copies ran while one was open for 2% of the time, Pallas kernels for 7%

profile of v1, /device:TPU:33, one launch (start us, length us, event | category | flops | bytes accessed | tf_op | source)
XLA Modules:
  0.0 129.8 jit_solution(3277188505999473365)
XLA Ops:
  0.0 0.0 copy-start.3
  0.0 0.0 copy-start.1
  0.0 0.0 copy-start.7
  0.0 1.7 %broadcast_in_dim.8 = f32[4,4,8,2,256]{4,3,2,1,0:T(2,128)} broadcast(f32[4,8,2,256]{3,2,1,0:T(2,128)} %bitcast.13), dimensions={0,2,3,4} | broadcast | bytes 327680 | tf_op jit(solution)/shard_map/broadcast_in_dim | solution.py:480
  1.7 12.8 %all-to-all-start = ((f32[128,2,256]{2,1,0:T(2,128)}), f32[128,2,256]{2,1,0:T(2,128)S(1)}, u32[]{:S(2)}, u32[]{:S(2)}) async-start(f32[128,2,256]{2,1,0:T(2,128)} %bitcast.4), calls=%async_computation | async-start | bytes 524288 | tf_op jit(solution)/shard_map/all_to_all | solution.py:470
  14.5 1.2 pad_maximum_fusion
  15.7 1.5 %collective-permute-start.1 = (f32[2,32,4,128]{3,2,1,0:T(4,128)S(1)}, f32[2,32,4,128]{3,2,1,0:T(4,128)S(1)}, u32[]{:S(2)}, u32[]{:S(2)}) collective-permute-start(f32[2,32,4,128]{3,2,1,0:T(4,128)S(1)} %get-tuple-element.13), channel_id=1, source_target_pairs={{0,2},{2,4},{4,6},{6,8},{8,10},{10,12},{12,14},{14,16},{16,18},{18... | collective-permute-start | bytes 393224 | tf_op jit(solution)/shard_map/ppermute | solution.py:488
  17.2 0.0 collective-permute-start
  17.2 0.7 constant_dynamic-slice_fusion
  17.9 4.2 %collective-permute-start.2 = (f32[8,256]{1,0:T(8,128)S(1)}, f32[8,256]{1,0:T(8,128)S(1)}, u32[]{:S(2)}, u32[]{:S(2)}) collective-permute-start(f32[8,256]{1,0:T(8,128)S(1)} %constant_dynamic-slice_fusion), channel_id=1, source_target_pairs={{0,1},{1,0},{2,3},{3,2},{4,5},{5,4},{6,7},{7,6},{8,9},{9,8},{10,11... | collective-permute-start | bytes 24584 | tf_op jit(solution)/shard_map/ppermute | solution.py:483
  22.1 0.1 pad_add_fusion.where
  22.2 0.0 collective-permute-done.1.lower
  22.2 0.3 collective-permute-done.upper
  22.5 0.0 copy-start
  22.5 1.0 copy-done
  23.5 0.0 copy-start.2
  23.5 1.0 copy-done.2
  24.6 1.5 %pack.1 = (f32[2,32,8,128]{3,2,1,0:T(8,128)S(1)}, f32[32,8,128]{2,1,0:T(8,128)S(1)}) custom-call(s32[3]{0:T(128)S(1)} %pad_add_fusion.where, f32[32,32,128]{2,1,0:T(8,128)S(1)} %copy-done, f32[32,32,128]{2,1,0:T(8,128)S(1)} %copy-done.2, f32[2,32,4,128]{3,2,1,0:T(4,128)S(1)} %collective-permute-done.upper, f32[2,32,4,128]{3,2,1,0:T(4,128)S(1)} %collective-permute-done.1.lower), custom_call_target="tpu_custom_call" | custom-call | flops 2000000 | bytes 1600000 | tf_op jit(solution)/shard_map/pack/pallas_call | solution.py:72
  26.0 1.6 %all-to-all-done = f32[128,2,256]{2,1,0:T(2,128)S(1)} async-done(((f32[128,2,256]{2,1,0:T(2,128)}), f32[128,2,256]{2,1,0:T(2,128)S(1)}, u32[]{:S(2)}, u32[]{:S(2)}) %all-to-all-start) | async-done | bytes 262176 | tf_op jit(solution)/shard_map/all_to_all | solution.py:470
  27.6 0.2 reshape.17.coefs
  27.8 0.0 collective-permute-done.2.beside
  27.8 0.0 copy-start.4
  27.8 0.9 copy-done.4
  28.7 4.2 %expand.1 = f32[32,48,128]{2,1,0:T(8,128)} custom-call(s32[3]{0:T(128)S(1)} %pad_add_fusion.where, f32[256,256]{1,0:T(8,128)S(1)} %reshape.17.coefs, f32[128,256]{1,0:T(8,128)S(1)} %copy-done.4, f32[8,256]{1,0:T(8,128)S(1)} %collective-permute-done.2.beside, f32[4096,256]{1,0:T(8,128)} %first_basis.3), custom_call_target="tpu_custom_call" | custom-call | flops 1056964608 | bytes 3000000 | tf_op jit(solution)/shard_map/expand/pallas_call | solution.py:137
  33.0 6.7 %all-to-all-start.1 = ((f32[32,48,128]{2,1,0:T(8,128)}), f32[32,48,128]{2,1,0:T(8,128)S(1)}, u32[]{:S(2)}, u32[]{:S(2)}) async-start(f32[32,48,128]{2,1,0:T(8,128)} %expand.1), calls=%async_computation.1 | async-start | bytes 1572864 | tf_op jit(solution)/shard_map/all_to_all | solution.py:470
  39.7 4.5 %collective-permute-start.3 = (f32[32,8,128]{2,1,0:T(8,128)S(1)}, f32[32,8,128]{2,1,0:T(8,128)S(1)}, u32[]{:S(2)}, u32[]{:S(2)}) collective-permute-start(f32[32,8,128]{2,1,0:T(8,128)S(1)} %get-tuple-element.12), channel_id=1, source_target_pairs={{0,1},{1,0},{2,3},{3,2},{4,5},{5,4},{6,7},{7,6},{8,9},{9,8},{10,11... | collective-permute-start | bytes 393224 | tf_op jit(solution)/shard_map/ppermute | solution.py:491
  44.2 0.0 copy-done.7
  44.2 0.1 copy.7.basis_z
  44.3 0.0 copy-start.5
  44.3 4.5 %collective-permute-done.3.strip = f32[32,8,128]{2,1,0:T(8,128)S(1)} collective-permute-done((f32[32,8,128]{2,1,0:T(8,128)S(1)}, f32[32,8,128]{2,1,0:T(8,128)S(1)}, u32[]{:S(2)}, u32[]{:S(2)}) %collective-permute-start.3) | collective-permute-done | bytes 131104 | tf_op jit(solution)/shard_map/ppermute | solution.py:491
  48.8 0.0 copy-done.3
  48.8 0.0 copy-done.1
  48.8 8.0 %statics.1.fields = f32[14,32,40,128]{3,2,1,0:T(8,128)} custom-call(s32[3]{0:T(128)S(1)} %pad_add_fusion.where, f32[32,32,128]{2,1,0:T(8,128)S(1)} %copy-done.1, f32[32,32,128]{2,1,0:T(8,128)S(1)} %copy-done.3, f32[2,32,8,128]{3,2,1,0:T(8,128)S(1)} %get-tuple-element.11.rows, f32[32,8,128]{2,1,0:T(8,128)S(1)} %collective-permute-done.3.strip), custom_call_target="tpu_custom_call" | custom-call | flops 20000000 | bytes 12000000 | tf_op jit(solution)/shard_map/statics/pallas_call | solution.py:235
  56.7 0.0 copy-start.6
  56.7 0.0 all-to-all-done.1.layers
  56.8 17.4 %on_grid.1 = f32[32,32,128]{2,1,0:T(8,128)S(1)} custom-call(s32[3]{0:T(128)S(1)} %pad_add_fusion.where, f32[32,16]{1,0:T(8,128)S(1)} %copy.7.basis_z, f32[32,48,128]{2,1,0:T(8,128)S(1)} %all-to-all-done.1.layers, f32[32,32,128]{2,1,0:T(8,128)S(1)} %copy-done.1, f32[14,32,40,128]{3,2,1,0:T(8,128)} %statics.1.fields), custom_call_target="tpu_custom_call" | custom-call | flops 100000000 | bytes 12000000 | tf_op jit(solution)/shard_map/on_grid/pallas_call | solution.py:403
  74.1 19.4 %all_to_all.25 = f32[32,32,128]{2,1,0:T(8,128)S(1)} all-to-all(f32[32,32,128]{2,1,0:T(8,128)S(1)} %on_grid.1), channel_id=1, replica_groups=mesh['y'=4,'zl'=4,'x'=4,'core'=2,'zh'=2] {'y','x','core'}, dimensions={0} | all-to-all | bytes 1048576 | tf_op jit(solution)/shard_map/all_to_all | solution.py:470
  93.5 0.0 copy-done.5
  93.5 3.4 %project.1 = f32[8,64,128]{2,1,0:T(8,128)S(1)} custom-call(s32[3]{0:T(128)S(1)} %pad_add_fusion.where, f32[1024,128]{1,0:T(8,128)S(1)} %bitcast.12, f32[128,256]{1,0:T(8,128)S(1)} %copy-done.5, f32[4096,256]{1,0:T(8,128)} %first_basis.3), custom_call_target="tpu_custom_call" | custom-call | flops 503316480 | bytes 2000000 | tf_op jit(solution)/shard_map/project/pallas_call | solution.py:452
  97.0 20.1 %all_to_all.26 = f32[8,64,128]{2,1,0:T(8,128)S(1)} all-to-all(f32[8,64,128]{2,1,0:T(8,128)S(1)} %project.1), channel_id=1, replica_groups=mesh['y'=4,'zl'=4,'x'=4,'core'=2,'zh'=2] {'zl','zh'}, dimensions={0} | all-to-all | bytes 524288 | tf_op jit(solution)/shard_map/all_to_all | solution.py:470
  117.1 0.6 reduce_sum.9
  117.7 4.0 %all-to-all-start.4 = ((f32[32,2,128]{2,1,0:T(2,128)}), f32[32,2,128]{2,1,0:T(2,128)S(1)}, u32[]{:S(2)}, u32[]{:S(2)}) async-start(f32[32,2,128]{2,1,0:T(2,128)} %bitcast.8), calls=%async_computation.4 | async-start | bytes 65536 | tf_op jit(solution)/shard_map/all_to_all | solution.py:470
  121.8 7.4 %all-to-all-done.4 = f32[32,2,128]{2,1,0:T(2,128)S(1)} async-done(((f32[32,2,128]{2,1,0:T(2,128)}), f32[32,2,128]{2,1,0:T(2,128)S(1)}, u32[]{:S(2)}, u32[]{:S(2)}) %all-to-all-start.4) | async-done | bytes 32800 | tf_op jit(solution)/shard_map/all_to_all | solution.py:470
  129.1 0.0 copy-done.6
  129.1 0.6 dynamic-slice_add_fusion
Async XLA Ops:
  0.0 48.8 %copy-start.3 = (f32[32,32,128]{2,1,0:T(8,128)S(1)}, f32[32,32,128]{2,1,0:T(8,128)}, u32[]{:S(2)}) copy-start(f32[32,32,128]{2,1,0:T(8,128)} %prs.3) | copy-start | bytes 1572868
  0.0 48.8 %copy-start.1 = (f32[32,32,128]{2,1,0:T(8,128)S(1)}, f32[32,32,128]{2,1,0:T(8,128)}, u32[]{:S(2)}) copy-start(f32[32,32,128]{2,1,0:T(8,128)} %kap.5) | copy-start | bytes 1572868
  0.0 44.2 %copy-start.7 = (f32[32,16]{0,1:T(8,128)S(1)}, f32[32,16]{0,1:T(8,128)}, u32[]{:S(2)}) copy-start(f32[32,16]{0,1:T(8,128)} %param.9) | copy-start | bytes 6148
  1.7 25.9 %all-to-all-start = ((f32[128,2,256]{2,1,0:T(2,128)}), f32[128,2,256]{2,1,0:T(2,128)S(1)}, u32[]{:S(2)}, u32[]{:S(2)}) async-start(f32[128,2,256]{2,1,0:T(2,128)} %bitcast.4), calls=%async_computation | async-start | bytes 524288 | tf_op jit(solution)/shard_map/all_to_all | solution.py:470
  15.7 6.5 %collective-permute-start.1 = (f32[2,32,4,128]{3,2,1,0:T(4,128)S(1)}, f32[2,32,4,128]{3,2,1,0:T(4,128)S(1)}, u32[]{:S(2)}, u32[]{:S(2)}) collective-permute-start(f32[2,32,4,128]{3,2,1,0:T(4,128)S(1)} %get-tuple-element.13), channel_id=1, source_target_pairs={{0,2},{2,4},{4,6},{6,8},{8,10},{10,12},{12,14},{14,16},{16,18},{18... | collective-permute-start | bytes 393224 | tf_op jit(solution)/shard_map/ppermute | solution.py:488
  17.2 5.3 %collective-permute-start = (f32[2,32,4,128]{3,2,1,0:T(4,128)S(1)}, f32[2,32,4,128]{3,2,1,0:T(4,128)S(1)}, u32[]{:S(2)}, u32[]{:S(2)}) collective-permute-start(f32[2,32,4,128]{3,2,1,0:T(4,128)S(1)} %get-tuple-element.14), channel_id=1, source_target_pairs={{2,0},{4,2},{6,4},{8,6},{10,8},{12,10},{14,12},{16,14},{18,16},{20... | collective-permute-start | bytes 393224 | tf_op jit(solution)/shard_map/ppermute | solution.py:487
  17.9 9.9 %collective-permute-start.2 = (f32[8,256]{1,0:T(8,128)S(1)}, f32[8,256]{1,0:T(8,128)S(1)}, u32[]{:S(2)}, u32[]{:S(2)}) collective-permute-start(f32[8,256]{1,0:T(8,128)S(1)} %constant_dynamic-slice_fusion), channel_id=1, source_target_pairs={{0,1},{1,0},{2,3},{3,2},{4,5},{5,4},{6,7},{7,6},{8,9},{9,8},{10,11... | collective-permute-start | bytes 24584 | tf_op jit(solution)/shard_map/ppermute | solution.py:483
  22.5 1.0 copy-start
  23.5 1.0 copy-start.2
  27.8 0.9 copy-start.4
  33.0 23.8 %all-to-all-start.1 = ((f32[32,48,128]{2,1,0:T(8,128)}), f32[32,48,128]{2,1,0:T(8,128)S(1)}, u32[]{:S(2)}, u32[]{:S(2)}) async-start(f32[32,48,128]{2,1,0:T(8,128)} %expand.1), calls=%async_computation.1 | async-start | bytes 1572864 | tf_op jit(solution)/shard_map/all_to_all | solution.py:470
  39.7 9.0 %collective-permute-start.3 = (f32[32,8,128]{2,1,0:T(8,128)S(1)}, f32[32,8,128]{2,1,0:T(8,128)S(1)}, u32[]{:S(2)}, u32[]{:S(2)}) collective-permute-start(f32[32,8,128]{2,1,0:T(8,128)S(1)} %get-tuple-element.12), channel_id=1, source_target_pairs={{0,1},{1,0},{2,3},{3,2},{4,5},{5,4},{6,7},{7,6},{8,9},{9,8},{10,11... | collective-permute-start | bytes 393224 | tf_op jit(solution)/shard_map/ppermute | solution.py:491
  44.3 49.3 %copy-start.5 = (f32[128,256]{1,0:T(8,128)S(1)}, f32[128,256]{1,0:T(8,128)}, u32[]{:S(2)}) copy-start(f32[128,256]{1,0:T(8,128)} %basis.3) | copy-start | bytes 393220
  56.7 72.4 %copy-start.6 = (f32[2,16,2,256]{3,2,1,0:T(2,128)S(1)}, f32[2,16,2,256]{3,2,1,0:T(2,128)}, u32[]{:S(2)}) copy-start(f32[2,16,2,256]{3,2,1,0:T(2,128)} %param.6) | copy-start | bytes 196612
  117.7 11.4 %all-to-all-start.4 = ((f32[32,2,128]{2,1,0:T(2,128)}), f32[32,2,128]{2,1,0:T(2,128)S(1)}, u32[]{:S(2)}, u32[]{:S(2)}) async-start(f32[32,2,128]{2,1,0:T(2,128)} %bitcast.8), calls=%async_computation.4 | async-start | bytes 65536 | tf_op jit(solution)/shard_map/all_to_all | solution.py:470

commit v2 on v1

--- a/solution.py
+++ b/solution.py
@@ -25,6 +25,7 @@
 PER_STEP = 16
 LAYER_STEP = 4
 STATIC_STEP = 8
+STATIC_PARTS = 4
 MODES = 256
 FIELDS = 14
 BLOCK = 8 * ROWS
@@ -77,8 +78,8 @@
         ),
         in_specs=[SMEM] + [VMEM] * 4,
         out_specs=(VMEM, VMEM),
-        compiler_params=params(52),
-        cost_estimate=pl.CostEstimate(flops=2_000_000, bytes_accessed=1_600_000, transcendentals=0),
+        compiler_params=params(61),
+        cost_estimate=pl.CostEstimate(flops=2_000_000, bytes_accessed=100_000_000, transcendentals=0),
         name="pack",
     )(where, kap, prs, upper, lower)
 
@@ -144,20 +145,32 @@
             pltpu.VMEM((4, BLOCK + 16, MODES), f32),
             pltpu.SemaphoreType.DMA((4, 3)),
         ],
-        compiler_params=params(52),
+        compiler_params=params(61),
         cost_estimate=pl.CostEstimate(
-            flops=6 * 2 * 256 * 256 * 1344, bytes_accessed=3_000_000, transcendentals=0
+            flops=6 * 2 * 256 * 256 * 1344, bytes_accessed=40_000_000, transcendentals=0
         ),
         name="expand",
     )(where, coefs, basis, beside, first_basis)
 
 
-def statics_kernel(where, kap, prs, rows, strip, out, built, pp, ph, sem):
+def statics_kernel(
+    where, kap, prs, rows, strip, first_basis, out, plane_rows, built, pp, ph, sems, row_sems
+):
     kk, kh, pxc, pxh, pyc, pyh, pzc, pzh, exc, exh, eyc, eyh, ezc, ezh = (
         built.at[n] for n in range(FIELDS)
     )
-    gx, zh = where[0], where[1]
+    gx, zh, zl = where[0], where[1], where[2]
     half = 0.5 * step_size * step_size
+    row_copies = [
+        pltpu.make_async_copy(
+            first_basis.at[pl.ds(pl.multiple_of((y * 4 + zl) * BLOCK, BLOCK), BLOCK)],
+            plane_rows.at[pl.ds(y * BLOCK, BLOCK)],
+            row_sems.at[y],
+        )
+        for y in range(4)
+    ]
+    for copy in row_copies:
+        copy.start()
 
     def place(i, carry):
         for j in range(STATIC_STEP):
@@ -186,69 +199,82 @@
     mask_h = jnp.where(last & (zh == 0), 0.0, 1.0).astype(f32)
     lowest, highest_row = jnp.where(gx == 0, HALO - 1, -1), jnp.where(gx == 127, HALO + ROWS - 1, -1)
 
-    for start in (0, 8, 16, 24, 31):
-        at, up = pl.ds(start, 8), pl.ds(start + 1, 8)
-        here = row + start
-        mask_x = jnp.where((here == lowest) | (here == highest_row), 0.0, 1.0).astype(f32)
-
-        def along_x(i, carry, at=at, up=up, mask_x=mask_x):
-            for j in range(STATIC_STEP):
-                z = i * STATIC_STEP + j
-                exc[z, at] = (half * mask_x) * (kk[z, at] + kk[z, up])
-                exh[z, at] = (half * mask_x) * (kh[z, at] + kh[z, up])
-                pxc[z, at] = (0.5 * mask_x) * (pp[z, up] - pp[z, at])
-                pxh[z, at] = (0.5 * mask_x) * (ph[z, up] - ph[z, at])
-            return carry
-
-        lax.fori_loop(0, DEPTH // STATIC_STEP, along_x, 0)
-
-    for start in (0, 8, 16, 24, 32):
-        at = pl.ds(start, 8)
-
-        def along_yz(i, carry, at=at):
-            for j in range(STATIC_STEP):
-                z = i * STATIC_STEP + j
-                later = jnp.minimum(z + 1, DEPTH - 1)
-                inside = jnp.where(z < DEPTH - 1, 1.0, 0.0).astype(f32)
-                c, h, p, q = kk[z, at], kh[z, at], pp[z, at], ph[z, at]
-                cn, hn = columns_on(c, h, last)
-                pn, qn = columns_on(p, q, last)
-                eyc[z, at] = (half * mask_c) * (c + cn)
-                eyh[z, at] = (half * mask_h) * (h + hn)
-                pyc[z, at] = (0.5 * mask_c) * (pn - p)
-                pyh[z, at] = (0.5 * mask_h) * (qn - q)
-                ezc[z, at] = (half * inside) * (c + kk[later, at])
-                ezh[z, at] = (half * inside) * (h + kh[later, at])
-                pzc[z, at] = (0.5 * inside) * (pp[later, at] - p)
-                pzh[z, at] = (0.5 * inside) * (ph[later, at] - q)
-            return carry
-
-        lax.fori_loop(0, DEPTH // STATIC_STEP, along_yz, 0)
-
-    copy = pltpu.make_async_copy(built, out, sem)
-    copy.start()
-    copy.wait()
-
-
-def statics(where, kap, prs, rows, strip):
+    copies = []
+    span = DEPTH // STATIC_PARTS
+    for part in range(STATIC_PARTS):
+        begin, end = part * span // STATIC_STEP, (part + 1) * span // STATIC_STEP
+        for start in (0, 8, 16, 24, 31):
+            at, up = pl.ds(start, 8), pl.ds(start + 1, 8)
+            here = row + start
+            mask_x = jnp.where((here == lowest) | (here == highest_row), 0.0, 1.0).astype(f32)
+
+            def along_x(i, carry, at=at, up=up, mask_x=mask_x):
+                for j in range(STATIC_STEP):
+                    z = i * STATIC_STEP + j
+                    exc[z, at] = (half * mask_x) * (kk[z, at] + kk[z, up])
+                    exh[z, at] = (half * mask_x) * (kh[z, at] + kh[z, up])
+                    pxc[z, at] = (0.5 * mask_x) * (pp[z, up] - pp[z, at])
+                    pxh[z, at] = (0.5 * mask_x) * (ph[z, up] - ph[z, at])
+                return carry
+
+            lax.fori_loop(begin, end, along_x, 0)
+
+        for start in (0, 8, 16, 24, 32):
+            at = pl.ds(start, 8)
+
+            def along_yz(i, carry, at=at):
+                for j in range(STATIC_STEP):
+                    z = i * STATIC_STEP + j
+                    later = jnp.minimum(z + 1, DEPTH - 1)
+                    inside = jnp.where(z < DEPTH - 1, 1.0, 0.0).astype(f32)
+                    c, h, p, q = kk[z, at], kh[z, at], pp[z, at], ph[z, at]
+                    cn, hn = columns_on(c, h, last)
+                    pn, qn = columns_on(p, q, last)
+                    eyc[z, at] = (half * mask_c) * (c + cn)
+                    eyh[z, at] = (half * mask_h) * (h + hn)
+                    pyc[z, at] = (0.5 * mask_c) * (pn - p)
+                    pyh[z, at] = (0.5 * mask_h) * (qn - q)
+                    ezc[z, at] = (half * inside) * (c + kk[later, at])
+                    ezh[z, at] = (half * inside) * (h + kh[later, at])
+                    pzc[z, at] = (0.5 * inside) * (pp[later, at] - p)
+                    pzh[z, at] = (0.5 * inside) * (ph[later, at] - q)
+                return carry
+
+            lax.fori_loop(begin, end, along_yz, 0)
+
+        copies.append(
+            pltpu.make_async_copy(
+                built.at[:, pl.ds(part * span, span)], out.at[:, pl.ds(part * span, span)], sems.at[part]
+            )
+        )
+        copies[-1].start()
+    for copy in copies + row_copies:
+        copy.wait()
+
+
+def statics(where, kap, prs, rows, strip, first_basis):
     field = (DEPTH, EXT_ROWS, COLS)
     return pl.pallas_call(
         statics_kernel,
-        out_shape=jax.ShapeDtypeStruct((FIELDS,) + field, f32),
-        in_specs=[SMEM] + [VMEM] * 4,
-        out_specs=HBM,
+        out_shape=(
+            jax.ShapeDtypeStruct((FIELDS,) + field, f32),
+            jax.ShapeDtypeStruct((4 * BLOCK, MODES), f32),
+        ),
+        in_specs=[SMEM] + [VMEM] * 4 + [HBM],
+        out_specs=(HBM, HBM),
         scratch_shapes=[
             pltpu.VMEM((FIELDS,) + field, f32),
             pltpu.VMEM(field, f32),
             pltpu.VMEM(field, f32),
-            pltpu.SemaphoreType.DMA,
+            pltpu.SemaphoreType.DMA((STATIC_PARTS,)),
+            pltpu.SemaphoreType.DMA((4,)),
         ],
         compiler_params=params(52),
         cost_estimate=pl.CostEstimate(
-            flops=20_000_000, bytes_accessed=12_000_000, transcendentals=0
+            flops=20_000_000, bytes_accessed=150_000_000, transcendentals=0
         ),
         name="statics",
-    )(where, kap, prs, rows, strip)
+    )(where, kap, prs, rows, strip, first_basis)
 
 
 def grid_kernel(where, basis_z, layers, kap, fields, out, built, uc, uh, vc, vh, sens, sems):
@@ -419,22 +445,9 @@
     )(where, basis_z, layers, kap, fields)
 
 
-def project_kernel(where, values, basis, first_basis, out, blocks, sems):
-    zl = where[2]
-    copies = []
-    for y in range(4):
-        start = pl.multiple_of((y * 4 + zl) * BLOCK, BLOCK)
-        copies.append(
-            pltpu.make_async_copy(
-                first_basis.at[pl.ds(start, BLOCK)], blocks.at[pl.ds(y * BLOCK, BLOCK)], sems.at[y]
-            )
-        )
-    for copy in copies:
-        copy.start()
-    for copy in copies:
-        copy.wait()
+def project_kernel(values, basis, plane_rows, out):
     along_x = lax.dot_general(
-        blocks[...], values[...], (((0,), (0,)), ((), ())),
+        plane_rows[...], values[...], (((0,), (0,)), ((), ())),
         precision=highest, preferred_element_type=f32,
     )
     full = lax.dot_general(
@@ -448,22 +461,18 @@
                 out[z * 2 + h, pl.ds(y * 16, 16)] = full[at : at + 16, h * 128 : (h + 1) * 128]
 
 
-def project(where, values, basis, first_basis):
+def project(values, basis, plane_rows):
     return pl.pallas_call(
         project_kernel,
         out_shape=jax.ShapeDtypeStruct((8, 64, 128), f32),
-        in_specs=[SMEM, VMEM, VMEM, HBM],
+        in_specs=[VMEM, VMEM, VMEM],
         out_specs=VMEM,
-        scratch_shapes=[
-            pltpu.VMEM((4 * BLOCK, MODES), f32),
-            pltpu.SemaphoreType.DMA((4,)),
-        ],
-        compiler_params=params(52),
+        compiler_params=params(48),
         cost_estimate=pl.CostEstimate(
             flops=6 * 2 * 256 * 128 * 1280, bytes_accessed=2_000_000, transcendentals=0
         ),
         name="project",
-    )(where, values, basis, first_basis)
+    )(values, basis, plane_rows)
 
 
 def exchanged(values, axes):
@@ -480,9 +489,8 @@
     spread = jnp.broadcast_to(flat.reshape(4, 1, 8, 2, MODES), (4, 4, 8, 2, MODES))
     gathered = exchanged(spread.reshape(128, 2, MODES), GX)
 
-    beside = lax.ppermute(
-        lax.dynamic_slice_in_dim(basis_y, (COLS - STRIP) * (1 - zh), STRIP, 0), "zh", swap
-    )
+    edges = jnp.concatenate([basis_y[:STRIP] * zh, basis_y[-STRIP:] * (1 - zh)])
+    beside = lax.psum_scatter(edges, "zh", scatter_dimension=0, tiled=True)
     both = jnp.stack([conductivity, pressure])
     upper = lax.ppermute(both[:, :, :HALO], GX, [((i + 1) % 128, i) for i in range(128)])
     lower = lax.ppermute(both[:, :, -HALO:], GX, [(i, (i + 1) % 128) for i in range(128)])
@@ -491,11 +499,12 @@
     strip = lax.ppermute(strip, "zh", swap)
 
     message = expand(where, gathered.reshape(MODES, MODES), basis_y, beside, first_axis_basis)
-    fields = statics(where, conductivity, pressure, rows, strip)
+    message, strip = lax.optimization_barrier((message, strip))
+    fields, plane_rows = statics(where, conductivity, pressure, rows, strip, first_axis_basis)
     layers = exchanged(message, PLANE)
     modes = on_grid(where, basis_z, layers, conductivity, fields)
     columns = exchanged(modes, PLANE)
-    shares = project(where, columns.reshape(4 * BLOCK, COLS), basis_y, first_axis_basis)
+    shares = project(columns.reshape(4 * BLOCK, COLS), basis_y, plane_rows)
     summed = jnp.sum(exchanged(shares, RING), axis=0)
     result = exchanged(summed.reshape(32, 2, 128), PLANE)
     own = lax.dynamic_slice_in_dim(coefficients, zh * 128, 128, 3)

time: 130 us -> 166 us (1.28)
  Pallas kernels: 34.4 us -> 60 us
  between operations: 0.13 us -> 13.5 us
  blocking collectives: 39.5 us -> 33 us
  waiting for transfers between devices: 13.8 us -> 19 us
  starting transfers between devices: 33.7 us -> 30.5 us
  other arithmetic: 2.49 us -> 4.32 us
    pallas_call x1, Pallas kernels: 7.97 us -> 33.5 us  [statics(): pl.pallas_call(statics_kernel, out_shape=(jax.ShapeDtypeStruct((FIELDS,)...]
    reduce_scatter x0 -> x1, waiting for transfers between devices: none -> 8.23 us  [per_device(): beside = lax.psum_scatter(edges, 'zh', scatter_dimension=0, tiled=True)]
    all_to_all x2, blocking collectives: 39.5 us -> 33 us  [exchanged(): return lax.all_to_all(values, axes, split_axis=0, concat_axis=0, tiled=True)]
    ppermute x1, waiting for transfers between devices: 4.48 us -> 0.01 us  [per_device(): strip = lax.ppermute(strip, 'zh', swap)]
    ppermute x1 -> x0, starting transfers between devices: 4.21 us -> none  [per_device(): lax.ppermute(lax.dynamic_slice_in_dim(basis_y, (COLS - STRIP) * (1 - zh),...]
    ppermute x1, waiting for transfers between devices: 0.33 us -> 2.78 us  [per_device(): lax.ppermute(both[:, :, :HALO], GX, [((i + 1) % 128, i) for i in range(12...]
    pallas_call x1, Pallas kernels: 3.44 us -> 1.66 us  [project(): pl.pallas_call(project_kernel, out_shape=jax.ShapeDtypeStruct((8, 64, 128...]
  transfers between devices with their start and end apart: 7 -> 7, of which waited for: 4 -> 4; matrix products, arithmetic and copies ran while one was open for 2% -> 2% of each run, Pallas kernels for 7% -> 25%
where the time goes in v2:
time: 166 us; the launch traced here: 165 us
  Pallas kernels  60 us (36%)
  blocking collectives  33 us (20%)
  starting transfers between devices  30.5 us (18%)
  waiting for transfers between devices  19 us (11%)
  between operations  13.5 us (8%)
  local copies, waits for them, and re-layouts  4.94 us (3%)
  other arithmetic  4.32 us (3%)
    pallas_call x1, Pallas kernels, statics(): pl.pallas_call(statics_kernel, out_shape=(jax.ShapeDtypeStruct((FIELDS,)...  33.5 us
    all_to_all x2, blocking collectives, exchanged(): return lax.all_to_all(values, axes, split_axis=0, concat_axis=0, tiled=True)  33 us
    all_to_all x3, starting transfers between devices, exchanged(): return lax.all_to_all(values, axes, split_axis=0, concat_axis=0, tiled=True)  24.7 us
    pallas_call x1, Pallas kernels, on_grid(): pl.pallas_call(grid_kernel, out_shape=jax.ShapeDtypeStruct((DIRECTIONS *...  17.4 us
    reduce_scatter x1, waiting for transfers between devices, per_device(): beside = lax.psum_scatter(edges, 'zh', scatter_dimension=0, tiled=True)  8.23 us
    all_to_all x3, waiting for transfers between devices, exchanged(): return lax.all_to_all(values, axes, split_axis=0, concat_axis=0, tiled=True)  7.36 us
    pallas_call x1, Pallas kernels, expand(): pl.pallas_call(expand_kernel, out_shape=jax.ShapeDtypeStruct((32, EXT_ROW...  4.63 us
    ppermute x1, starting transfers between devices, per_device(): strip = lax.ppermute(strip, 'zh', swap)  4.21 us
  transfers between devices with their start and end apart: 7, of which 4 were waited for; matrix products, arithmetic and copies ran while one was open for 2% of the time, Pallas kernels for 25%

profile of v2, /device:TPU:33, one launch (start us, length us, event | category | flops | bytes accessed | tf_op | source)
XLA Modules:
  0.0 165.2 jit_solution(17587203261683202070)
XLA Ops:
  6.5 0.0 copy-start.1
  6.5 0.0 copy-start
  6.5 0.0 copy-start.9
  6.5 1.8 %broadcast_in_dim.8 = f32[4,4,8,2,256]{4,3,2,1,0:T(2,128)} broadcast(f32[4,8,2,256]{3,2,1,0:T(2,128)} %bitcast.13), dimensions={0,2,3,4} | broadcast | bytes 327680 | tf_op jit(solution)/shard_map/broadcast_in_dim | solution.py:489
  8.3 12.8 %all-to-all-start = ((f32[128,2,256]{2,1,0:T(2,128)}), f32[128,2,256]{2,1,0:T(2,128)S(1)}, u32[]{:S(2)}, u32[]{:S(2)}) async-start(f32[128,2,256]{2,1,0:T(2,128)} %bitcast.4), calls=%async_computation | async-start | bytes 524288 | tf_op jit(solution)/shard_map/all_to_all | solution.py:479
  21.1 0.0 reduce-scatter.2.cloned.1.call-start
  21.1 1.2 pad_maximum_fusion
  22.3 1.5 collective-permute-start.1
  23.8 0.0 collective-permute-start
  23.8 0.7 slice_multiply_fusion.1
  24.5 0.6 pad_maximum_fusion.2
  25.1 0.0 reduce-scatter.2.cloned.1.call-update
  25.1 0.6 pad_add_fusion.where
  25.7 0.6 collective-permute-done.1.lower
  26.3 0.0 copy-start.7
  26.3 2.8 %collective-permute-done.upper = f32[2,32,4,128]{3,2,1,0:T(4,128)S(1)} collective-permute-done((f32[2,32,4,128]{3,2,1,0:T(4,128)S(1)}, f32[2,32,4,128]{3,2,1,0:T(4,128)S(1)}, u32[]{:S(2)}, u32[]{:S(2)}) %collective-permute-start) | collective-permute-done | bytes 131104 | tf_op jit(solution)/shard_map/ppermute | solution.py:495
  29.1 0.0 copy-done.7
  29.1 0.0 copy-start.8
  29.1 0.7 copy-done.8
  29.7 2.8 %pack.1 = (f32[2,32,8,128]{3,2,1,0:T(8,128)}, f32[32,8,128]{2,1,0:T(8,128)}) custom-call(s32[3]{0:T(128)} %pad_add_fusion.where, f32[32,32,128]{2,1,0:T(8,128)} %kap.5, f32[32,32,128]{2,1,0:T(8,128)} %prs.3, f32[2,32,4,128]{3,2,1,0:T(4,128)} %copy-done.8, f32[2,32,4,128]{3,2,1,0:T(4,128)} %copy-done.7), custom_call_target="tpu_custom_call" | custom-call | flops 2000000 | bytes 100000000 | tf_op jit(solution)/shard_map/pack/pallas_call | solution.py:73
  32.6 4.2 %collective-permute-start.2 = (f32[32,8,128]{2,1,0:T(8,128)}, f32[32,8,128]{2,1,0:T(8,128)S(1)}, u32[]{:S(2)}, u32[]{:S(2)}) collective-permute-start(f32[32,8,128]{2,1,0:T(8,128)} %get-tuple-element.15), channel_id=1, source_target_pairs={{0,1},{1,0},{2,3},{3,2},{4,5},{5,4},{6,7},{7,6},{8,9},{9,8},{10,11... | collective-permute-start | bytes 393224 | tf_op jit(solution)/shard_map/ppermute | solution.py:499
  36.8 0.0 all-to-all-done
  36.8 0.9 reshape.17.coefs
  37.7 8.2 %reduce-scatter.2.cloned.1.call-done.beside = f32[8,256]{1,0:T(8,128)} async-done(((f32[16,256]{1,0:T(8,128)}), f32[8,256]{1,0:T(8,128)}) %reduce-scatter.2.cloned.1.call-update) | async-done | bytes 8208 | tf_op jit(solution)/shard_map/reduce_scatter | solution.py:493
  45.9 4.6 %expand.1 = f32[32,48,128]{2,1,0:T(8,128)} custom-call(s32[3]{0:T(128)} %pad_add_fusion.where, f32[256,256]{1,0:T(8,128)} %reshape.17.coefs, f32[128,256]{1,0:T(8,128)} %basis.3, f32[8,256]{1,0:T(8,128)} %reduce-scatter.2.cloned.1.call-done.beside, f32[4096,256]{1,0:T(8,128)} %first_basis.3), custom_call_target="tpu_custom_call" | custom-call | flops 1056964608 | bytes 40000000 | tf_op jit(solution)/shard_map/expand/pallas_call | solution.py:138
  50.6 0.0 collective-permute-done.2.strip
  50.6 8.0 %all-to-all-start.1 = ((f32[32,48,128]{2,1,0:T(8,128)}), f32[32,48,128]{2,1,0:T(8,128)S(1)}, u32[]{:S(2)}, u32[]{:S(2)}) async-start(f32[32,48,128]{2,1,0:T(8,128)} %expand.1), calls=%async_computation.2 | async-start | bytes 1572864 | tf_op jit(solution)/shard_map/all_to_all | solution.py:479
  58.5 0.0 copy-done.9
  58.6 0.0 copy-start.3
  58.6 0.1 copy.7.basis_z
  58.6 0.0 copy-done.1
  58.6 0.0 copy-done
  58.6 0.0 copy-start.4
  58.7 0.9 copy-done.4
  59.6 0.0 copy-start.5
  59.6 0.6 copy-done.5
  60.2 0.0 copy-start.6
  60.2 33.5 %statics.1 = (f32[14,32,40,128]{3,2,1,0:T(8,128)}, f32[1024,256]{1,0:T(8,128)}) custom-call(s32[3]{0:T(128)S(1)} %copy-done.5, f32[32,32,128]{2,1,0:T(8,128)S(1)} %copy-done, f32[32,32,128]{2,1,0:T(8,128)S(1)} %copy-done.1, f32[2,32,8,128]{3,2,1,0:T(8,128)S(1)} %copy-done.4, f32[32,8,128]{2,1,0:T(8,128)S(1)} %collective-permute-done.2.strip, ...), custom_call_target="tpu_custom_call" | custom-call | flops 20000000 | bytes 150000000 | tf_op jit(solution)/shard_map/statics/pallas_call | solution.py:257
  93.7 0.0 copy-start.2
  93.7 0.0 all-to-all-done.1.layers
  93.7 17.4 %on_grid.1 = f32[32,32,128]{2,1,0:T(8,128)S(1)} custom-call(s32[3]{0:T(128)S(1)} %copy-done.5, f32[32,16]{1,0:T(8,128)S(1)} %copy.7.basis_z, f32[32,48,128]{2,1,0:T(8,128)S(1)} %all-to-all-done.1.layers, f32[32,32,128]{2,1,0:T(8,128)S(1)} %copy-done, f32[14,32,40,128]{3,2,1,0:T(8,128)} %get-tuple-element.19.fields), custom_call_target="tpu_custom_call" | custom-call | flops 100000000 | bytes 12000000 | tf_op jit(solution)/shard_map/on_grid/pallas_call | solution.py:429
  111.1 18.7 %all_to_all.25 = f32[32,32,128]{2,1,0:T(8,128)S(1)} all-to-all(f32[32,32,128]{2,1,0:T(8,128)S(1)} %on_grid.1), channel_id=1, replica_groups=mesh['y'=4,'zl'=4,'x'=4,'core'=2,'zh'=2] {'y','x','core'}, dimensions={0} | all-to-all | bytes 1048576 | tf_op jit(solution)/shard_map/all_to_all | solution.py:479
  129.8 0.0 copy-done.3
  129.8 0.0 copy-done.2
  129.8 1.7 %project.1 = f32[8,64,128]{2,1,0:T(8,128)S(1)} custom-call(f32[1024,128]{1,0:T(8,128)S(1)} %bitcast.12, f32[128,256]{1,0:T(8,128)S(1)} %copy-done.3, f32[1024,256]{1,0:T(8,128)S(1)} %copy-done.2), custom_call_target="tpu_custom_call" | custom-call | flops 503316480 | bytes 2000000 | tf_op jit(solution)/shard_map/project/pallas_call | solution.py:465
  131.5 14.3 %all_to_all.26 = f32[8,64,128]{2,1,0:T(8,128)S(1)} all-to-all(f32[8,64,128]{2,1,0:T(8,128)S(1)} %project.1), channel_id=1, replica_groups=mesh['y'=4,'zl'=4,'x'=4,'core'=2,'zh'=2] {'zl','zh'}, dimensions={0} | all-to-all | bytes 524288 | tf_op jit(solution)/shard_map/all_to_all | solution.py:479
  145.7 0.6 reduce_sum.9
  146.4 4.0 %all-to-all-start.4 = ((f32[32,2,128]{2,1,0:T(2,128)}), f32[32,2,128]{2,1,0:T(2,128)S(1)}, u32[]{:S(2)}, u32[]{:S(2)}) async-start(f32[32,2,128]{2,1,0:T(2,128)} %bitcast.8), calls=%async_computation.5 | async-start | bytes 65536 | tf_op jit(solution)/shard_map/all_to_all | solution.py:479
  150.4 7.4 %all-to-all-done.4 = f32[32,2,128]{2,1,0:T(2,128)S(1)} async-done(((f32[32,2,128]{2,1,0:T(2,128)}), f32[32,2,128]{2,1,0:T(2,128)S(1)}, u32[]{:S(2)}, u32[]{:S(2)}) %all-to-all-start.4) | async-done | bytes 32800 | tf_op jit(solution)/shard_map/all_to_all | solution.py:479
  157.7 0.0 copy-done.6
  157.7 0.6 dynamic-slice_add_fusion
Async XLA Ops:
  6.5 52.1 %copy-start.1 = (f32[32,32,128]{2,1,0:T(8,128)S(1)}, f32[32,32,128]{2,1,0:T(8,128)}, u32[]{:S(2)}) copy-start(f32[32,32,128]{2,1,0:T(8,128)} %prs.3) | copy-start | bytes 1572868
  6.5 52.1 %copy-start = (f32[32,32,128]{2,1,0:T(8,128)S(1)}, f32[32,32,128]{2,1,0:T(8,128)}, u32[]{:S(2)}) copy-start(f32[32,32,128]{2,1,0:T(8,128)} %kap.5) | copy-start | bytes 1572868
  6.5 52.0 %copy-start.9 = (f32[32,16]{0,1:T(8,128)S(1)}, f32[32,16]{0,1:T(8,128)}, u32[]{:S(2)}) copy-start(f32[32,16]{0,1:T(8,128)} %param.9) | copy-start | bytes 6148
  8.3 28.5 %all-to-all-start = ((f32[128,2,256]{2,1,0:T(2,128)}), f32[128,2,256]{2,1,0:T(2,128)S(1)}, u32[]{:S(2)}, u32[]{:S(2)}) async-start(f32[128,2,256]{2,1,0:T(2,128)} %bitcast.4), calls=%async_computation | async-start | bytes 524288 | tf_op jit(solution)/shard_map/all_to_all | solution.py:479
  21.1 24.9 %reduce-scatter.2.cloned.1.call-start = ((), (), s32[]{:S(2)}) async-start(), calls=%async_computation.6 | async-start | bytes 24576 | tf_op jit(solution)/shard_map/reduce_scatter | solution.py:493
  22.3 4.0 %collective-permute-start.1 = (f32[2,32,4,128]{3,2,1,0:T(4,128)S(1)}, f32[2,32,4,128]{3,2,1,0:T(4,128)S(1)}, u32[]{:S(2)}, u32[]{:S(2)}) collective-permute-start(f32[2,32,4,128]{3,2,1,0:T(4,128)S(1)} %get-tuple-element.21), channel_id=1, source_target_pairs={{0,2},{2,4},{4,6},{6,8},{8,10},{10,12},{12,14},{14,16},{16,18},{18... | collective-permute-start | bytes 393224 | tf_op jit(solution)/shard_map/ppermute | solution.py:496
  23.8 5.3 %collective-permute-start = (f32[2,32,4,128]{3,2,1,0:T(4,128)S(1)}, f32[2,32,4,128]{3,2,1,0:T(4,128)S(1)}, u32[]{:S(2)}, u32[]{:S(2)}) collective-permute-start(f32[2,32,4,128]{3,2,1,0:T(4,128)S(1)} %get-tuple-element.22), channel_id=1, source_target_pairs={{2,0},{4,2},{6,4},{8,6},{10,8},{12,10},{14,12},{16,14},{18,16},{20... | collective-permute-start | bytes 393224 | tf_op jit(solution)/shard_map/ppermute | solution.py:495
  26.3 2.8 %copy-start.7 = (f32[2,32,4,128]{3,2,1,0:T(4,128)}, f32[2,32,4,128]{3,2,1,0:T(4,128)S(1)}, u32[]{:S(2)}) copy-start(f32[2,32,4,128]{3,2,1,0:T(4,128)S(1)} %collective-permute-done.1.lower) | copy-start | bytes 393220
  29.1 0.7 copy-start.8
  32.6 18.0 %collective-permute-start.2 = (f32[32,8,128]{2,1,0:T(8,128)}, f32[32,8,128]{2,1,0:T(8,128)S(1)}, u32[]{:S(2)}, u32[]{:S(2)}) collective-permute-start(f32[32,8,128]{2,1,0:T(8,128)} %get-tuple-element.15), channel_id=1, source_target_pairs={{0,1},{1,0},{2,3},{3,2},{4,5},{5,4},{6,7},{7,6},{8,9},{9,8},{10,11... | collective-permute-start | bytes 393224 | tf_op jit(solution)/shard_map/ppermute | solution.py:499
  50.6 43.1 %all-to-all-start.1 = ((f32[32,48,128]{2,1,0:T(8,128)}), f32[32,48,128]{2,1,0:T(8,128)S(1)}, u32[]{:S(2)}, u32[]{:S(2)}) async-start(f32[32,48,128]{2,1,0:T(8,128)} %expand.1), calls=%async_computation.2 | async-start | bytes 1572864 | tf_op jit(solution)/shard_map/all_to_all | solution.py:479
  58.6 71.2 %copy-start.3 = (f32[128,256]{1,0:T(8,128)S(1)}, f32[128,256]{1,0:T(8,128)}, u32[]{:S(2)}) copy-start(f32[128,256]{1,0:T(8,128)} %basis.3) | copy-start | bytes 393220
  58.6 1.0 copy-start.4
  59.6 0.6 copy-start.5
  60.2 97.5 %copy-start.6 = (f32[2,16,2,256]{3,2,1,0:T(2,128)S(1)}, f32[2,16,2,256]{3,2,1,0:T(2,128)}, u32[]{:S(2)}) copy-start(f32[2,16,2,256]{3,2,1,0:T(2,128)} %param.6) | copy-start | bytes 196612
  93.7 36.1 %copy-start.2 = (f32[1024,256]{1,0:T(8,128)S(1)}, f32[1024,256]{1,0:T(8,128)}, u32[]{:S(2)}) copy-start(f32[1024,256]{1,0:T(8,128)} %get-tuple-element.20.plane_rows) | copy-start | bytes 3145732
  146.4 11.4 %all-to-all-start.4 = ((f32[32,2,128]{2,1,0:T(2,128)}), f32[32,2,128]{2,1,0:T(2,128)S(1)}, u32[]{:S(2)}, u32[]{:S(2)}) async-start(f32[32,2,128]{2,1,0:T(2,128)} %bitcast.8), calls=%async_computation.5 | async-start | bytes 65536 | tf_op jit(solution)/shard_map/all_to_all | solution.py:479
Sparse Core Ops, SparseCore 0:
  25.2 20.6 reduce-scatter.1

commit v3 on v2

--- a/solution.py
+++ b/solution.py
@@ -47,7 +47,7 @@
     return jnp.where(last, h, c), jnp.where(last, c, h)
 
 
-def pack_kernel(where, kap, prs, upper, lower, rows_out, strip_out):
+def pack_kernel(where, kap, prs, basis, out):
     zh = where[1]
     lane = lax.broadcasted_iota(jnp.int32, (STRIP, COLS), 1)
 
@@ -56,32 +56,33 @@
             z = i * LAYER_STEP + j
             packed = jnp.zeros((STRIP, COLS), f32)
             for f, ref in enumerate((kap, prs)):
-                beside = jnp.concatenate([upper[f, z], lower[f, z]], axis=0)
-                rows_out[f, z] = beside
-                for g in range(GROUPS):
-                    tile = ref[z, pl.ds(8 * g, 8)] if g < ROWS // 8 else beside
-                    first = f * EXT_ROWS + 8 * g
-                    moved = pltpu.roll(tile, lax.rem(first + 8 * (1 - zh), COLS), 1)
+                for g in range(ROWS // 8):
+                    first = f * ROWS + 8 * g
+                    moved = pltpu.roll(
+                        ref[z, pl.ds(8 * g, 8)], lax.rem(first + 8 * (1 - zh), COLS), 1
+                    )
                     packed = jnp.where((lane >= first) & (lane < first + 8), moved, packed)
-            strip_out[z] = packed
+            out[z] = packed
         return carry
 
     lax.fori_loop(0, DEPTH // LAYER_STEP, body, 0)
-
-
-def pack(where, kap, prs, upper, lower):
+    edge = jnp.where(zh == 0, basis[COLS - STRIP :], basis[:STRIP])
+    for part in range(2):
+        out[DEPTH + part] = edge[:, COLS * part : COLS * (part + 1)]
+
+
+def pack(where, kap, prs, basis):
     return pl.pallas_call(
         pack_kernel,
-        out_shape=(
-            jax.ShapeDtypeStruct((2, DEPTH, 2 * HALO, COLS), f32),
-            jax.ShapeDtypeStruct((DEPTH, STRIP, COLS), f32),
-        ),
-        in_specs=[SMEM] + [VMEM] * 4,
-        out_specs=(VMEM, VMEM),
+        out_shape=jax.ShapeDtypeStruct((DEPTH + 2, STRIP, COLS), f32),
+        in_specs=[SMEM] + [VMEM] * 3,
+        out_specs=VMEM,
         compiler_params=params(61),
-        cost_estimate=pl.CostEstimate(flops=2_000_000, bytes_accessed=100_000_000, transcendentals=0),
+        cost_estimate=pl.CostEstimate(
+            flops=2_000_000, bytes_accessed=1_300_000, transcendentals=0
+        ),
         name="pack",
-    )(where, kap, prs, upper, lower)
+    )(where, kap, prs, basis)
 
 
 def expand_kernel(where, coefs, basis, beside, first_basis, out, wide, blocks, sems):
@@ -104,7 +105,8 @@
     for copy in copies:
         copy.start()
     wide[pl.ds(0, COLS)] = basis[...]
-    wide[pl.ds(COLS, STRIP)] = beside[...]
+    for part in range(2):
+        wide[pl.ds(COLS, STRIP), pl.ds(COLS * part, COLS)] = beside[DEPTH + part]
     wide[pl.ds(COLS + STRIP, COLS - STRIP)] = jnp.zeros((COLS - STRIP, MODES), f32)
     columns = lax.dot_general(
         coefs[...], wide[...], (((1,), (1,)), ((), ())),
@@ -154,7 +156,8 @@
 
 
 def statics_kernel(
-    where, kap, prs, rows, strip, first_basis, out, plane_rows, built, pp, ph, sems, row_sems
+    where, kap, prs, upper, lower, strip, first_basis, out, plane_rows,
+    built, pp, ph, held, sems, row_sems,
 ):
     kk, kh, pxc, pxh, pyc, pyh, pzc, pzh, exc, exh, eyc, eyh, ezc, ezh = (
         built.at[n] for n in range(FIELDS)
@@ -164,7 +167,7 @@
     row_copies = [
         pltpu.make_async_copy(
             first_basis.at[pl.ds(pl.multiple_of((y * 4 + zl) * BLOCK, BLOCK), BLOCK)],
-            plane_rows.at[pl.ds(y * BLOCK, BLOCK)],
+            held.at[pl.ds(y * BLOCK, BLOCK)],
             row_sems.at[y],
         )
         for y in range(4)
@@ -177,17 +180,17 @@
             z = i * STATIC_STEP + j
             packed = strip[z]
             for f, (src, dst, far) in enumerate(((kap, kk, kh), (prs, pp, ph))):
-                ends = rows[f, z]
+                low, high = pl.ds(0, HALO), pl.ds(HALO + ROWS, HALO)
                 dst[z, pl.ds(HALO, ROWS)] = src[z]
-                dst[z, pl.ds(0, HALO)] = ends[HALO:]
-                dst[z, pl.ds(HALO + ROWS, HALO)] = ends[:HALO]
-                for g in range(GROUPS):
-                    tile = pltpu.roll(packed, strip_shift(zh, f * EXT_ROWS + 8 * g), 1)
-                    if g < ROWS // 8:
-                        far[z, pl.ds(HALO + 8 * g, 8)] = tile
-                    else:
-                        far[z, pl.ds(0, HALO)] = tile[HALO:]
-                        far[z, pl.ds(HALO + ROWS, HALO)] = tile[:HALO]
+                dst[z, low] = lower[f, z]
+                dst[z, high] = upper[f, z]
+                for g in range(ROWS // 8):
+                    far[z, pl.ds(HALO + 8 * g, 8)] = pltpu.roll(
+                        packed, strip_shift(zh, f * ROWS + 8 * g), 1
+                    )
+                corners = jnp.concatenate([lower[2, z], upper[2, z]], axis=0)
+                far[z, low] = pltpu.roll(corners, strip_shift(zh, (f + 1) * ROWS - 8), 1)[:HALO]
+                far[z, high] = pltpu.roll(corners, strip_shift(zh, f * ROWS), 1)[HALO:]
         return carry
 
     lax.fori_loop(0, DEPTH // STATIC_STEP, place, 0)
@@ -248,11 +251,15 @@
             )
         )
         copies[-1].start()
-    for copy in copies + row_copies:
+    for copy in row_copies:
         copy.wait()
-
-
-def statics(where, kap, prs, rows, strip, first_basis):
+    copies.append(pltpu.make_async_copy(held, plane_rows, row_sems.at[4]))
+    copies[-1].start()
+    for copy in copies:
+        copy.wait()
+
+
+def statics(where, kap, prs, upper, lower, strip, first_basis):
     field = (DEPTH, EXT_ROWS, COLS)
     return pl.pallas_call(
         statics_kernel,
@@ -260,21 +267,22 @@
             jax.ShapeDtypeStruct((FIELDS,) + field, f32),
             jax.ShapeDtypeStruct((4 * BLOCK, MODES), f32),
         ),
-        in_specs=[SMEM] + [VMEM] * 4 + [HBM],
+        in_specs=[SMEM] + [VMEM] * 5 + [HBM],
         out_specs=(HBM, HBM),
         scratch_shapes=[
             pltpu.VMEM((FIELDS,) + field, f32),
             pltpu.VMEM(field, f32),
             pltpu.VMEM(field, f32),
+            pltpu.VMEM((4 * BLOCK, MODES), f32),
             pltpu.SemaphoreType.DMA((STATIC_PARTS,)),
-            pltpu.SemaphoreType.DMA((4,)),
+            pltpu.SemaphoreType.DMA((5,)),
         ],
         compiler_params=params(52),
         cost_estimate=pl.CostEstimate(
             flops=20_000_000, bytes_accessed=150_000_000, transcendentals=0
         ),
         name="statics",
-    )(where, kap, prs, rows, strip, first_basis)
+    )(where, kap, prs, upper, lower, strip, first_basis)
 
 
 def grid_kernel(where, basis_z, layers, kap, fields, out, built, uc, uh, vc, vh, sens, sems):
@@ -489,18 +497,17 @@
     spread = jnp.broadcast_to(flat.reshape(4, 1, 8, 2, MODES), (4, 4, 8, 2, MODES))
     gathered = exchanged(spread.reshape(128, 2, MODES), GX)
 
-    edges = jnp.concatenate([basis_y[:STRIP] * zh, basis_y[-STRIP:] * (1 - zh)])
-    beside = lax.psum_scatter(edges, "zh", scatter_dimension=0, tiled=True)
+    strip = lax.ppermute(pack(where, conductivity, pressure, basis_y), "zh", [(0, 1), (1, 0)])
     both = jnp.stack([conductivity, pressure])
-    upper = lax.ppermute(both[:, :, :HALO], GX, [((i + 1) % 128, i) for i in range(128)])
-    lower = lax.ppermute(both[:, :, -HALO:], GX, [(i, (i + 1) % 128) for i in range(128)])
-    rows, strip = pack(where, conductivity, pressure, upper, lower)
-    gathered, rows = lax.optimization_barrier((gathered, rows))
-    strip = lax.ppermute(strip, "zh", swap)
-
-    message = expand(where, gathered.reshape(MODES, MODES), basis_y, beside, first_axis_basis)
-    message, strip = lax.optimization_barrier((message, strip))
-    fields, plane_rows = statics(where, conductivity, pressure, rows, strip, first_axis_basis)
+    heads = jnp.concatenate([both[:, :, :HALO], strip[None, :DEPTH, :HALO]])
+    tails = jnp.concatenate([both[:, :, -HALO:], strip[None, :DEPTH, -HALO:]])
+    upper = lax.ppermute(heads, GX, [(i + 1, i) for i in range(127)])
+    lower = lax.ppermute(tails, GX, [(i, i + 1) for i in range(127)])
+    message = expand(where, gathered.reshape(MODES, MODES), basis_y, strip, first_axis_basis)
+    message, upper, lower = lax.optimization_barrier((message, upper, lower))
+    fields, plane_rows = statics(
+        where, conductivity, pressure, upper, lower, strip, first_axis_basis
+    )
     layers = exchanged(message, PLANE)
     modes = on_grid(where, basis_z, layers, conductivity, fields)
     columns = exchanged(modes, PLANE)

time: 166 us -> 122 us (0.73)
  Pallas kernels: 60 us -> 32 us
  between operations: 13.5 us -> 0.17 us
  waiting for transfers between devices: 19 us -> 21.1 us
  blocking collectives: 33 us -> 31.3 us
    pallas_call x1, Pallas kernels: 33.5 us -> 5.52 us  [statics(): pl.pallas_call(statics_kernel, out_shape=(jax.ShapeDtypeStruct((FIELDS,)...]
    all_to_all x3, waiting for transfers between devices: 7.36 us -> 21.1 us  [exchanged(): return lax.all_to_all(values, axes, split_axis=0, concat_axis=0, tiled=True)]
    reduce_scatter x1 -> x0, waiting for transfers between devices: 8.23 us -> none  [per_device(): beside = lax.psum_scatter(edges, 'zh', scatter_dimension=0, tiled=True)]
    ppermute x3, starting transfers between devices: 5.72 us -> 11.3 us  [the longest x1 6.01 us: per_device(): lax.ppermute(pack(where, conductivity, pressure, basis_y), 'zh', [(0, 1),...]
    all_to_all x3, starting transfers between devices: 24.7 us -> 19.4 us  [exchanged(): return lax.all_to_all(values, axes, split_axis=0, concat_axis=0, tiled=True)]
    ppermute x3, waiting for transfers between devices: 3.37 us -> 0.01 us  [the longest x1 0.01 us: per_device(): lax.ppermute(pack(where, conductivity, pressure, basis_y), 'zh', [(0, 1),...]
    all_to_all x2, blocking collectives: 33 us -> 31.3 us  [exchanged(): return lax.all_to_all(values, axes, split_axis=0, concat_axis=0, tiled=True)]
  transfers between devices with their start and end apart: 7 -> 6, of which waited for: 4 -> 3; matrix products, arithmetic and copies ran while one was open for 2% -> 3% of each run, Pallas kernels for 25% -> 8%
where the time goes in v3:
time: 122 us
  Pallas kernels  32 us (26%)
  blocking collectives  31.3 us (26%)
  starting transfers between devices  30.6 us (25%)
  waiting for transfers between devices  21.1 us (17%)
  local copies, waits for them, and re-layouts  3.57 us (3%)
  other arithmetic  3.09 us (3%)
    all_to_all x2, blocking collectives, exchanged(): return lax.all_to_all(values, axes, split_axis=0, concat_axis=0, tiled=True)  31.3 us
    all_to_all x3, waiting for transfers between devices, exchanged(): return lax.all_to_all(values, axes, split_axis=0, concat_axis=0, tiled=True)  21.1 us
    all_to_all x3, starting transfers between devices, exchanged(): return lax.all_to_all(values, axes, split_axis=0, concat_axis=0, tiled=True)  19.4 us
    pallas_call x1, Pallas kernels, on_grid(): pl.pallas_call(grid_kernel, out_shape=jax.ShapeDtypeStruct((DIRECTIONS *...  17.4 us
    ppermute x1, starting transfers between devices, per_device(): lax.ppermute(pack(where, conductivity, pressure, basis_y), 'zh', [(0, 1),...  6.01 us
    pallas_call x1, Pallas kernels, statics(): pl.pallas_call(statics_kernel, out_shape=(jax.ShapeDtypeStruct((FIELDS,)...  5.52 us
    pallas_call x1, Pallas kernels, expand(): pl.pallas_call(expand_kernel, out_shape=jax.ShapeDtypeStruct((32, EXT_ROW...  4.66 us
    ppermute x1, starting transfers between devices, per_device(): lower = lax.ppermute(tails, GX, [(i, i + 1) for i in range(127)])  3.34 us
  transfers between devices with their start and end apart: 6, of which 3 were waited for; matrix products, arithmetic and copies ran while one was open for 3% of the time, Pallas kernels for 8%

profile of v3, /device:TPU:33, one launch (start us, length us, event | category | flops | bytes accessed | tf_op | source)
XLA Modules:
  0.0 121.9 jit_solution(2359943641680769885)
XLA Ops:
  0.0 0.0 copy-start
  0.0 0.0 copy-start.1
  0.0 0.0 copy-start.8
  0.0 0.6 pad_add_fusion.where
  0.6 0.0 copy-start.6
  0.6 2.7 %pack.1 = f32[34,8,128]{2,1,0:T(8,128)} custom-call(s32[3]{0:T(128)} %pad_add_fusion.where, f32[32,32,128]{2,1,0:T(8,128)} %kap.5, f32[32,32,128]{2,1,0:T(8,128)} %prs.3, f32[128,256]{1,0:T(8,128)} %basis.5), custom_call_target="tpu_custom_call" | custom-call | flops 2000000 | bytes 1300000 | tf_op jit(solution)/shard_map/pack/pallas_call | solution.py:75
  3.4 6.0 %collective-permute-start = (f32[34,8,128]{2,1,0:T(8,128)}, f32[34,8,128]{2,1,0:T(8,128)S(1)}, u32[]{:S(2)}, u32[]{:S(2)}) collective-permute-start(f32[34,8,128]{2,1,0:T(8,128)} %pack.1), channel_id=1, source_target_pairs={{0,1},{1,0},{2,3},{3,2},{4,5},{5,4},{6,7},{7,6},{8,9},{9,8},{10,11... | collective-permute-start | bytes 417800 | tf_op jit(solution)/shard_map/ppermute | solution.py:500
  9.4 1.7 %broadcast_in_dim.14 = f32[4,4,8,2,256]{4,3,2,1,0:T(2,128)} broadcast(f32[4,8,2,256]{3,2,1,0:T(2,128)} %bitcast.17), dimensions={0,2,3,4} | broadcast | bytes 327680 | tf_op jit(solution)/shard_map/broadcast_in_dim | solution.py:497
  11.0 11.2 %all-to-all-start = ((f32[128,2,256]{2,1,0:T(2,128)}), f32[128,2,256]{2,1,0:T(2,128)S(1)}, u32[]{:S(2)}, u32[]{:S(2)}) async-start(f32[128,2,256]{2,1,0:T(2,128)} %bitcast.4), calls=%async_computation | async-start | bytes 524288 | tf_op jit(solution)/shard_map/all_to_all | solution.py:487
  22.3 0.0 collective-permute-done.beside.strip
  22.3 0.0 copy-start.2
  22.3 1.2 fusion
  23.5 3.3 %collective-permute-start.2 = (f32[3,32,4,128]{3,2,1,0:T(4,128)S(1)}, f32[3,32,4,128]{3,2,1,0:T(4,128)S(1)}, u32[]{:S(2)}, u32[]{:S(2)}) collective-permute-start(f32[3,32,4,128]{3,2,1,0:T(4,128)S(1)} %get-tuple-element.15), channel_id=1, source_target_pairs={{0,2},{2,4},{4,6},{6,8},{8,10},{10,12},{12,14},{14,16},{16,18},{18... | collective-permute-start | bytes 589832 | tf_op jit(solution)/shard_map/ppermute | solution.py:505
  26.9 1.9 %collective-permute-start.1 = (f32[3,32,4,128]{3,2,1,0:T(4,128)S(1)}, f32[3,32,4,128]{3,2,1,0:T(4,128)S(1)}, u32[]{:S(2)}, u32[]{:S(2)}) collective-permute-start(f32[3,32,4,128]{3,2,1,0:T(4,128)S(1)} %get-tuple-element.16), channel_id=1, source_target_pairs={{2,0},{4,2},{6,4},{8,6},{10,8},{12,10},{14,12},{16,14},{18,16},{20... | collective-permute-start | bytes 589832 | tf_op jit(solution)/shard_map/ppermute | solution.py:504
  28.8 5.9 %all-to-all-done = f32[128,2,256]{2,1,0:T(2,128)S(1)} async-done(((f32[128,2,256]{2,1,0:T(2,128)}), f32[128,2,256]{2,1,0:T(2,128)S(1)}, u32[]{:S(2)}, u32[]{:S(2)}) %all-to-all-start) | async-done | bytes 262176 | tf_op jit(solution)/shard_map/all_to_all | solution.py:487
  34.7 0.9 reshape.17.coefs
  35.6 0.0 copy-done.2
  35.6 4.7 %expand.1 = f32[32,48,128]{2,1,0:T(8,128)} custom-call(s32[3]{0:T(128)} %pad_add_fusion.where, f32[256,256]{1,0:T(8,128)} %reshape.17.coefs, f32[128,256]{1,0:T(8,128)} %basis.5, f32[34,8,128]{2,1,0:T(8,128)} %copy-done.2, f32[4096,256]{1,0:T(8,128)} %first_basis.3), custom_call_target="tpu_custom_call" | custom-call | flops 1056964608 | bytes 40000000 | tf_op jit(solution)/shard_map/expand/pallas_call | solution.py:140
  40.3 0.0 collective-permute-done.2.lower
  40.3 0.0 collective-permute-done.1.upper
  40.3 4.1 %all-to-all-start.1 = ((f32[32,48,128]{2,1,0:T(8,128)}), f32[32,48,128]{2,1,0:T(8,128)S(1)}, u32[]{:S(2)}, u32[]{:S(2)}) async-start(f32[32,48,128]{2,1,0:T(8,128)} %expand.1), calls=%async_computation.1 | async-start | bytes 1572864 | tf_op jit(solution)/shard_map/all_to_all | solution.py:487
  44.5 0.0 copy-done.8
  44.5 0.1 copy.7.basis_z
  44.5 0.0 copy-done
  44.5 0.0 copy-done.1
  44.6 0.0 copy-done.6
  44.6 0.0 copy-start.3
  44.6 0.9 copy-done.3
  45.5 0.0 copy-start.4
  45.5 0.0 copy-start.7
  45.5 5.5 %statics.1 = (f32[14,32,40,128]{3,2,1,0:T(8,128)}, f32[1024,256]{1,0:T(8,128)}) custom-call(s32[3]{0:T(128)S(1)} %copy-done.6, f32[32,32,128]{2,1,0:T(8,128)S(1)} %copy-done, f32[32,32,128]{2,1,0:T(8,128)S(1)} %copy-done.1, f32[3,32,4,128]{3,2,1,0:T(4,128)S(1)} %collective-permute-done.1.upper, f32[3,32,4,128]{3,2,1,0:T(4,128)S(1)} %collective-permute-done.2.lower, ...), custom_call_target="tpu_custom_call" | custom-call | flops 20000000 | bytes 150000000 | tf_op jit(solution)/shard_map/statics/pallas_call | solution.py:264
  51.0 0.0 copy-start.5
  51.0 7.8 %all-to-all-done.1.layers = f32[32,48,128]{2,1,0:T(8,128)S(1)} async-done(((f32[32,48,128]{2,1,0:T(8,128)}), f32[32,48,128]{2,1,0:T(8,128)S(1)}, u32[]{:S(2)}, u32[]{:S(2)}) %all-to-all-start.1) | async-done | bytes 786464 | tf_op jit(solution)/shard_map/all_to_all | solution.py:487
  58.8 17.4 %on_grid.1 = f32[32,32,128]{2,1,0:T(8,128)S(1)} custom-call(s32[3]{0:T(128)S(1)} %copy-done.6, f32[32,16]{1,0:T(8,128)S(1)} %copy.7.basis_z, f32[32,48,128]{2,1,0:T(8,128)S(1)} %all-to-all-done.1.layers, f32[32,32,128]{2,1,0:T(8,128)S(1)} %copy-done, f32[14,32,40,128]{3,2,1,0:T(8,128)} %get-tuple-element.13.fields), custom_call_target="tpu_custom_call" | custom-call | flops 100000000 | bytes 12000000 | tf_op jit(solution)/shard_map/on_grid/pallas_call | solution.py:437
  76.2 15.2 %all_to_all.25 = f32[32,32,128]{2,1,0:T(8,128)S(1)} all-to-all(f32[32,32,128]{2,1,0:T(8,128)S(1)} %on_grid.1), channel_id=1, replica_groups=mesh['y'=4,'zl'=4,'x'=4,'core'=2,'zh'=2] {'y','x','core'}, dimensions={0} | all-to-all | bytes 1048576 | tf_op jit(solution)/shard_map/all_to_all | solution.py:487
  91.4 0.0 copy-done.4
  91.4 0.0 copy-done.5
  91.4 1.7 %project.1 = f32[8,64,128]{2,1,0:T(8,128)S(1)} custom-call(f32[1024,128]{1,0:T(8,128)S(1)} %bitcast.16, f32[128,256]{1,0:T(8,128)S(1)} %copy-done.4, f32[1024,256]{1,0:T(8,128)S(1)} %copy-done.5), custom_call_target="tpu_custom_call" | custom-call | flops 503316480 | bytes 2000000 | tf_op jit(solution)/shard_map/project/pallas_call | solution.py:473
  93.1 16.2 %all_to_all.26 = f32[8,64,128]{2,1,0:T(8,128)S(1)} all-to-all(f32[8,64,128]{2,1,0:T(8,128)S(1)} %project.1), channel_id=1, replica_groups=mesh['y'=4,'zl'=4,'x'=4,'core'=2,'zh'=2] {'zl','zh'}, dimensions={0} | all-to-all | bytes 524288 | tf_op jit(solution)/shard_map/all_to_all | solution.py:487
  109.2 0.6 reduce_sum.9
  109.9 4.0 %all-to-all-start.4 = ((f32[32,2,128]{2,1,0:T(2,128)}), f32[32,2,128]{2,1,0:T(2,128)S(1)}, u32[]{:S(2)}, u32[]{:S(2)}) async-start(f32[32,2,128]{2,1,0:T(2,128)} %bitcast.10), calls=%async_computation.4 | async-start | bytes 65536 | tf_op jit(solution)/shard_map/all_to_all | solution.py:487
  113.9 7.4 %all-to-all-done.4 = f32[32,2,128]{2,1,0:T(2,128)S(1)} async-done(((f32[32,2,128]{2,1,0:T(2,128)}), f32[32,2,128]{2,1,0:T(2,128)S(1)}, u32[]{:S(2)}, u32[]{:S(2)}) %all-to-all-start.4) | async-done | bytes 32800 | tf_op jit(solution)/shard_map/all_to_all | solution.py:487
  121.2 0.0 copy-done.7
  121.2 0.6 dynamic-slice_add_fusion
  (1 shorter events, 0.0 us)
Async XLA Ops:
  0.0 44.5 %copy-start = (f32[32,32,128]{2,1,0:T(8,128)S(1)}, f32[32,32,128]{2,1,0:T(8,128)}, u32[]{:S(2)}) copy-start(f32[32,32,128]{2,1,0:T(8,128)} %kap.5) | copy-start | bytes 1572868
  0.0 44.5 %copy-start.1 = (f32[32,32,128]{2,1,0:T(8,128)S(1)}, f32[32,32,128]{2,1,0:T(8,128)}, u32[]{:S(2)}) copy-start(f32[32,32,128]{2,1,0:T(8,128)} %prs.3) | copy-start | bytes 1572868
  0.0 44.5 %copy-start.8 = (f32[32,16]{0,1:T(8,128)S(1)}, f32[32,16]{0,1:T(8,128)}, u32[]{:S(2)}) copy-start(f32[32,16]{0,1:T(8,128)} %param.9) | copy-start | bytes 6148
  0.6 43.9 %copy-start.6 = (s32[3]{0:T(128)S(1)}, s32[3]{0:T(128)}, u32[]{:S(2)}) copy-start(s32[3]{0:T(128)} %pad_add_fusion.where) | copy-start | bytes 40
  3.4 18.9 %collective-permute-start = (f32[34,8,128]{2,1,0:T(8,128)}, f32[34,8,128]{2,1,0:T(8,128)S(1)}, u32[]{:S(2)}, u32[]{:S(2)}) collective-permute-start(f32[34,8,128]{2,1,0:T(8,128)} %pack.1), channel_id=1, source_target_pairs={{0,1},{1,0},{2,3},{3,2},{4,5},{5,4},{6,7},{7,6},{8,9},{9,8},{10,11... | collective-permute-start | bytes 417800 | tf_op jit(solution)/shard_map/ppermute | solution.py:500
  11.0 23.7 %all-to-all-start = ((f32[128,2,256]{2,1,0:T(2,128)}), f32[128,2,256]{2,1,0:T(2,128)S(1)}, u32[]{:S(2)}, u32[]{:S(2)}) async-start(f32[128,2,256]{2,1,0:T(2,128)} %bitcast.4), calls=%async_computation | async-start | bytes 524288 | tf_op jit(solution)/shard_map/all_to_all | solution.py:487
  22.3 13.3 %copy-start.2 = (f32[34,8,128]{2,1,0:T(8,128)}, f32[34,8,128]{2,1,0:T(8,128)S(1)}, u32[]{:S(2)}) copy-start(f32[34,8,128]{2,1,0:T(8,128)S(1)} %collective-permute-done.beside.strip) | copy-start | bytes 417796
  23.5 16.8 %collective-permute-start.2 = (f32[3,32,4,128]{3,2,1,0:T(4,128)S(1)}, f32[3,32,4,128]{3,2,1,0:T(4,128)S(1)}, u32[]{:S(2)}, u32[]{:S(2)}) collective-permute-start(f32[3,32,4,128]{3,2,1,0:T(4,128)S(1)} %get-tuple-element.15), channel_id=1, source_target_pairs={{0,2},{2,4},{4,6},{6,8},{8,10},{10,12},{12,14},{14,16},{16,18},{18... | collective-permute-start | bytes 589832 | tf_op jit(solution)/shard_map/ppermute | solution.py:505
  26.9 13.4 %collective-permute-start.1 = (f32[3,32,4,128]{3,2,1,0:T(4,128)S(1)}, f32[3,32,4,128]{3,2,1,0:T(4,128)S(1)}, u32[]{:S(2)}, u32[]{:S(2)}) collective-permute-start(f32[3,32,4,128]{3,2,1,0:T(4,128)S(1)} %get-tuple-element.16), channel_id=1, source_target_pairs={{2,0},{4,2},{6,4},{8,6},{10,8},{12,10},{14,12},{16,14},{18,16},{20... | collective-permute-start | bytes 589832 | tf_op jit(solution)/shard_map/ppermute | solution.py:504
  40.3 18.5 %all-to-all-start.1 = ((f32[32,48,128]{2,1,0:T(8,128)}), f32[32,48,128]{2,1,0:T(8,128)S(1)}, u32[]{:S(2)}, u32[]{:S(2)}) async-start(f32[32,48,128]{2,1,0:T(8,128)} %expand.1), calls=%async_computation.1 | async-start | bytes 1572864 | tf_op jit(solution)/shard_map/all_to_all | solution.py:487
  44.6 0.9 copy-start.3
  45.5 45.9 %copy-start.4 = (f32[128,256]{1,0:T(8,128)S(1)}, f32[128,256]{1,0:T(8,128)}, u32[]{:S(2)}) copy-start(f32[128,256]{1,0:T(8,128)} %basis.5) | copy-start | bytes 393220
  45.5 75.8 %copy-start.7 = (f32[2,16,2,256]{3,2,1,0:T(2,128)S(1)}, f32[2,16,2,256]{3,2,1,0:T(2,128)}, u32[]{:S(2)}) copy-start(f32[2,16,2,256]{3,2,1,0:T(2,128)} %param.6) | copy-start | bytes 196612
  51.0 40.4 %copy-start.5 = (f32[1024,256]{1,0:T(8,128)S(1)}, f32[1024,256]{1,0:T(8,128)}, u32[]{:S(2)}) copy-start(f32[1024,256]{1,0:T(8,128)} %get-tuple-element.14.plane_rows) | copy-start | bytes 3145732
  109.9 11.4 %all-to-all-start.4 = ((f32[32,2,128]{2,1,0:T(2,128)}), f32[32,2,128]{2,1,0:T(2,128)S(1)}, u32[]{:S(2)}, u32[]{:S(2)}) async-start(f32[32,2,128]{2,1,0:T(2,128)} %bitcast.10), calls=%async_computation.4 | async-start | bytes 65536 | tf_op jit(solution)/shard_map/all_to_all | solution.py:487

commit v4 on v3

--- a/solution.py
+++ b/solution.py
@@ -34,6 +34,12 @@
 HBM = pl.BlockSpec(memory_space=pltpu.HBM)
 
 
+def place_in_grid():
+    zl = lax.axis_index("zl")
+    plane = lax.axis_index("x") * 2 + lax.axis_index("core")
+    return (lax.axis_index("y") * 4 + zl) * 8 + plane, lax.axis_index("zh"), zl
+
+
 def params(mib):
     return pltpu.CompilerParams(vmem_limit_bytes=mib * 1024 * 1024)
 
@@ -47,8 +53,13 @@
     return jnp.where(last, h, c), jnp.where(last, c, h)
 
 
-def pack_kernel(where, kap, prs, basis, out):
-    zh = where[1]
+def pack_kernel(coefs, kap, prs, basis, spread, out):
+    _, zh, _ = place_in_grid()
+    for y in range(4):
+        for part in range(4):
+            values = coefs[pl.ds(8 * y, 8), part // 2, pl.ds(COLS * (part % 2), COLS)]
+            for zl in range(4):
+                spread[pl.ds((y * 4 + zl) * 32 + part, 8, stride=4), :] = values
     lane = lax.broadcasted_iota(jnp.int32, (STRIP, COLS), 1)
 
     def body(i, carry):
@@ -71,22 +82,25 @@
         out[DEPTH + part] = edge[:, COLS * part : COLS * (part + 1)]
 
 
-def pack(where, kap, prs, basis):
+def pack(coefs, kap, prs, basis):
     return pl.pallas_call(
         pack_kernel,
-        out_shape=jax.ShapeDtypeStruct((DEPTH + 2, STRIP, COLS), f32),
-        in_specs=[SMEM] + [VMEM] * 3,
-        out_specs=VMEM,
+        out_shape=(
+            jax.ShapeDtypeStruct((512, COLS), f32),
+            jax.ShapeDtypeStruct((DEPTH + 2, STRIP, COLS), f32),
+        ),
+        in_specs=[VMEM] * 4,
+        out_specs=(VMEM, VMEM),
         compiler_params=params(61),
         cost_estimate=pl.CostEstimate(
-            flops=2_000_000, bytes_accessed=1_300_000, transcendentals=0
+            flops=2_000_000, bytes_accessed=100_000_000, transcendentals=0
         ),
         name="pack",
-    )(where, kap, prs, basis)
-
-
-def expand_kernel(where, coefs, basis, beside, first_basis, out, wide, blocks, sems):
-    zl = where[2]
+    )(coefs, kap, prs, basis)
+
+
+def expand_kernel(coefs, basis, beside, first_basis, out, wide, blocks, sems):
+    _, _, zl = place_in_grid()
     copies = []
     for y in range(4):
         start = pl.multiple_of((y * 4 + zl) * BLOCK, BLOCK)
@@ -108,8 +122,11 @@
     for part in range(2):
         wide[pl.ds(COLS, STRIP), pl.ds(COLS * part, COLS)] = beside[DEPTH + part]
     wide[pl.ds(COLS + STRIP, COLS - STRIP)] = jnp.zeros((COLS - STRIP, MODES), f32)
+    modes = jnp.concatenate(
+        [coefs[pl.ds(part, MODES, stride=2), :] for part in range(2)], axis=1
+    )
     columns = lax.dot_general(
-        coefs[...], wide[...], (((1,), (1,)), ((), ())),
+        modes, wide[...], (((1,), (1,)), ((), ())),
         precision=highest, preferred_element_type=f32,
     )
     lane = lax.broadcasted_iota(jnp.int32, (STRIP, COLS), 1)
@@ -136,11 +153,11 @@
             out[q, pl.ds(EXT_ROWS, STRIP)] = packed
 
 
-def expand(where, coefs, basis, beside, first_basis):
+def expand(coefs, basis, beside, first_basis):
     return pl.pallas_call(
         expand_kernel,
         out_shape=jax.ShapeDtypeStruct((32, EXT_ROWS + STRIP, COLS), f32),
-        in_specs=[SMEM, VMEM, VMEM, VMEM, HBM],
+        in_specs=[VMEM, VMEM, VMEM, HBM],
         out_specs=VMEM,
         scratch_shapes=[
             pltpu.VMEM((EXT_COLS, MODES), f32),
@@ -152,17 +169,17 @@
             flops=6 * 2 * 256 * 256 * 1344, bytes_accessed=40_000_000, transcendentals=0
         ),
         name="expand",
-    )(where, coefs, basis, beside, first_basis)
+    )(coefs, basis, beside, first_basis)
 
 
 def statics_kernel(
-    where, kap, prs, upper, lower, strip, first_basis, out, plane_rows,
+    kap, prs, upper, lower, strip, first_basis, out, plane_rows,
     built, pp, ph, held, sems, row_sems,
 ):
     kk, kh, pxc, pxh, pyc, pyh, pzc, pzh, exc, exh, eyc, eyh, ezc, ezh = (
         built.at[n] for n in range(FIELDS)
     )
-    gx, zh, zl = where[0], where[1], where[2]
+    gx, zh, zl = place_in_grid()
     half = 0.5 * step_size * step_size
     row_copies = [
         pltpu.make_async_copy(
@@ -259,7 +276,7 @@
         copy.wait()
 
 
-def statics(where, kap, prs, upper, lower, strip, first_basis):
+def statics(kap, prs, upper, lower, strip, first_basis):
     field = (DEPTH, EXT_ROWS, COLS)
     return pl.pallas_call(
         statics_kernel,
@@ -267,7 +284,7 @@
             jax.ShapeDtypeStruct((FIELDS,) + field, f32),
             jax.ShapeDtypeStruct((4 * BLOCK, MODES), f32),
         ),
-        in_specs=[SMEM] + [VMEM] * 5 + [HBM],
+        in_specs=[VMEM] * 5 + [HBM],
         out_specs=(HBM, HBM),
         scratch_shapes=[
             pltpu.VMEM((FIELDS,) + field, f32),
@@ -282,10 +299,10 @@
             flops=20_000_000, bytes_accessed=150_000_000, transcendentals=0
         ),
         name="statics",
-    )(where, kap, prs, upper, lower, strip, first_basis)
-
-
-def grid_kernel(where, basis_z, layers, kap, fields, out, built, uc, uh, vc, vh, sens, sems):
+    )(kap, prs, upper, lower, strip, first_basis)
+
+
+def grid_kernel(basis_z, layers, kap, fields, out, built, uc, uh, vc, vh, sens, sems):
     kk, kh, pxc, pxh, pyc, pyh, pzc, pzh, exc, exh, eyc, eyh, ezc, ezh = (
         built.at[n] for n in range(FIELDS)
     )
@@ -298,7 +315,7 @@
     for copy in copies:
         copy.start()
     copies[0].wait()
-    zh = where[1]
+    _, zh, _ = place_in_grid()
     lane = lax.broadcasted_iota(jnp.int32, (8, COLS), 1)
     first, last = lane == 0, lane == COLS - 1
     tiles = (EXT_ROWS + STRIP) // 8
@@ -349,21 +366,17 @@
                 for j in range(PER_STEP):
                     z = i * PER_STEP + j
                     later = jnp.minimum(z + 1, DEPTH - 1)
+                    nxc, nxh, bxc, bxh = axc[z, at], axh[z, at], axc[z, down], axh[z, down]
+                    nyc, nyh, nzc, nzh = ayc[z, at], ayh[z, at], azc[z, at], azh[z, at]
                     for d in range(DIRECTIONS):
                         c, h, fzc, fzh = carry[4 * d : 4 * d + 4]
                         cz, hz = src_c[d, later, at], src_h[d, later, at]
                         cy, hy = columns_on(c, h, last)
-                        fyc, fyh = join(cy, c) * ayc[z, at], join(hy, h) * ayh[z, at]
+                        fyc, fyh = join(cy, c) * nyc, join(hy, h) * nyh
                         byc, byh = columns_back(fyc, fyh)
-                        gzc, gzh = join(cz, c) * azc[z, at], join(hz, h) * azh[z, at]
-                        xc = (
-                            join(src_c[d, z, up], c) * axc[z, at]
-                            - join(c, src_c[d, z, down]) * axc[z, down]
-                        )
-                        xh = (
-                            join(src_h[d, z, up], h) * axh[z, at]
-                            - join(h, src_h[d, z, down]) * axh[z, down]
-                        )
+                        gzc, gzh = join(cz, c) * nzc, join(hz, h) * nzh
+                        xc = join(src_c[d, z, up], c) * nxc - join(c, src_c[d, z, down]) * bxc
+                        xh = join(src_h[d, z, up], h) * nxh - join(h, src_h[d, z, down]) * bxh
                         total_c = xc + (fyc - byc) + (gzc - fzc)
                         total_h = xh + (fyh - byh) + (gzh - fzh)
                         if scale is not None:
@@ -403,16 +416,20 @@
             for j in range(PER_STEP):
                 z = i * PER_STEP + j
                 later = jnp.minimum(z + 1, DEPTH - 1)
+                nxc, bxc, nyc, nyh, nzc = (
+                    pxc[z, at], pxc[z, down], pyc[z, at], pyh[z, at], pzc[z, at]
+                )
+                weight = -kap[z, own]
                 for d in range(DIRECTIONS):
                     c, fzc = carry[2 * d : 2 * d + 2]
                     h = vh[d, z, at]
                     cz = vc[d, later, at]
                     cy, hy = columns_on(c, h, last)
-                    fyc, fyh = (cy - c) * pyc[z, at], (hy - h) * pyh[z, at]
+                    fyc, fyh = (cy - c) * nyc, (hy - h) * nyh
                     byc, _ = columns_back(fyc, fyh)
-                    gzc = (cz - c) * pzc[z, at]
-                    xc = (vc[d, z, up] - c) * pxc[z, at] + (c - vc[d, z, down]) * pxc[z, down]
-                    sens[d, z, own] = -kap[z, own] * (xc + (fyc + byc) + (gzc + fzc))
+                    gzc = (cz - c) * nzc
+                    xc = (vc[d, z, up] - c) * nxc + (c - vc[d, z, down]) * bxc
+                    sens[d, z, own] = weight * (xc + (fyc + byc) + (gzc + fzc))
                     carry[2 * d : 2 * d + 2] = [cz, gzc]
             return tuple(carry)
 
@@ -432,12 +449,12 @@
     lax.fori_loop(0, MODES_Z, modes_of, 0)
 
 
-def on_grid(where, basis_z, layers, kap, fields):
+def on_grid(basis_z, layers, kap, fields):
     wide = (DIRECTIONS, DEPTH, EXT_ROWS, COLS)
     return pl.pallas_call(
         grid_kernel,
         out_shape=jax.ShapeDtypeStruct((DIRECTIONS * MODES_Z, ROWS, COLS), f32),
-        in_specs=[SMEM, SMEM, VMEM, VMEM, HBM],
+        in_specs=[SMEM, VMEM, VMEM, HBM],
         out_specs=VMEM,
         scratch_shapes=[pltpu.VMEM((FIELDS, DEPTH, EXT_ROWS, COLS), f32)]
         + [pltpu.VMEM(wide, f32) for _ in range(4)]
@@ -450,7 +467,7 @@
             flops=100_000_000, bytes_accessed=12_000_000, transcendentals=0
         ),
         name="on_grid",
-    )(where, basis_z, layers, kap, fields)
+    )(basis_z, layers, kap, fields)
 
 
 def project_kernel(values, basis, plane_rows, out):
@@ -488,28 +505,21 @@
 
 
 def per_device(coefficients, first_axis_basis, basis_y, basis_z, conductivity, pressure):
-    gx = lax.axis_index(GX)
     zh = lax.axis_index("zh")
-    where = jnp.stack([gx, zh, lax.axis_index("zl")]).astype(jnp.int32)
-    swap = [(0, 1), (1, 0)]
-
     flat = coefficients.reshape(DIRECTIONS * MODES_Z, 2, MODES)
-    spread = jnp.broadcast_to(flat.reshape(4, 1, 8, 2, MODES), (4, 4, 8, 2, MODES))
-    gathered = exchanged(spread.reshape(128, 2, MODES), GX)
-
-    strip = lax.ppermute(pack(where, conductivity, pressure, basis_y), "zh", [(0, 1), (1, 0)])
+    spread, strip = pack(flat, conductivity, pressure, basis_y)
+    gathered = exchanged(spread.reshape(128, 4, COLS), GX)
+    strip = lax.ppermute(strip, "zh", [(0, 1), (1, 0)])
     both = jnp.stack([conductivity, pressure])
     heads = jnp.concatenate([both[:, :, :HALO], strip[None, :DEPTH, :HALO]])
     tails = jnp.concatenate([both[:, :, -HALO:], strip[None, :DEPTH, -HALO:]])
     upper = lax.ppermute(heads, GX, [(i + 1, i) for i in range(127)])
     lower = lax.ppermute(tails, GX, [(i, i + 1) for i in range(127)])
-    message = expand(where, gathered.reshape(MODES, MODES), basis_y, strip, first_axis_basis)
+    message = expand(gathered.reshape(512, COLS), basis_y, strip, first_axis_basis)
     message, upper, lower = lax.optimization_barrier((message, upper, lower))
-    fields, plane_rows = statics(
-        where, conductivity, pressure, upper, lower, strip, first_axis_basis
-    )
+    fields, plane_rows = statics(conductivity, pressure, upper, lower, strip, first_axis_basis)
     layers = exchanged(message, PLANE)
-    modes = on_grid(where, basis_z, layers, conductivity, fields)
+    modes = on_grid(basis_z, layers, conductivity, fields)
     columns = exchanged(modes, PLANE)
     shares = project(columns.reshape(4 * BLOCK, COLS), basis_y, plane_rows)
     summed = jnp.sum(exchanged(shares, RING), axis=0)

time: 122 us -> 122 us (level)
  local copies, waits for them, and re-layouts: 3.57 us -> 1.72 us
  blocking collectives: 31.3 us -> 32.7 us
    broadcast_in_dim x1 -> x0, local copies, waits for them, and re-layouts: 1.66 us -> none  [per_device(): jnp.broadcast_to(flat.reshape(4, 1, 8, 2, MODES), (4, 4, 8, 2, MODES))]
    all_to_all x2, blocking collectives: 31.3 us -> 32.7 us  [exchanged(): return lax.all_to_all(values, axes, split_axis=0, concat_axis=0, tiled=True)]
  transfers between devices with their start and end apart: 6 -> 6, of which waited for: 3 -> 3; matrix products, arithmetic and copies ran while one was open for 3% -> 1% of each run, Pallas kernels for 8% -> 8%
where the time goes in v4:
time: 122 us; the launch traced here: 121 us
  blocking collectives  32.7 us (27%)
  Pallas kernels  32.1 us (26%)
  starting transfers between devices  30.8 us (25%)
  waiting for transfers between devices  21.2 us (17%)
  other arithmetic  2.48 us (2%)
  local copies, waits for them, and re-layouts  1.72 us (1%)
    all_to_all x2, blocking collectives, exchanged(): return lax.all_to_all(values, axes, split_axis=0, concat_axis=0, tiled=True)  32.7 us
    all_to_all x3, waiting for transfers between devices, exchanged(): return lax.all_to_all(values, axes, split_axis=0, concat_axis=0, tiled=True)  21.2 us
    all_to_all x3, starting transfers between devices, exchanged(): return lax.all_to_all(values, axes, split_axis=0, concat_axis=0, tiled=True)  19.2 us
    pallas_call x1, Pallas kernels, on_grid(): pl.pallas_call(grid_kernel, out_shape=jax.ShapeDtypeStruct((DIRECTIONS *...  18 us
    ppermute x1, starting transfers between devices, per_device(): strip = lax.ppermute(strip, 'zh', [(0, 1), (1, 0)])  6.01 us
    pallas_call x1, Pallas kernels, statics(): pl.pallas_call(statics_kernel, out_shape=(jax.ShapeDtypeStruct((FIELDS,)...  4.95 us
    pallas_call x1, Pallas kernels, expand(): pl.pallas_call(expand_kernel, out_shape=jax.ShapeDtypeStruct((32, EXT_ROW...  4.64 us
    ppermute x1, starting transfers between devices, per_device(): lower = lax.ppermute(tails, GX, [(i, i + 1) for i in range(127)])  3.29 us
  transfers between devices with their start and end apart: 6, of which 3 were waited for; matrix products, arithmetic and copies ran while one was open for 1% of the time, Pallas kernels for 8%

profile of v4, /device:TPU:33, one launch (start us, length us, event | category | flops | bytes accessed | tf_op | source)
XLA Modules:
  0.0 121.2 jit_solution(16097591334151038130)
XLA Ops:
  0.0 0.0 copy-start
  0.0 0.0 copy-start.1
  0.0 0.0 copy-start.8
  0.0 2.9 %pack.1 = (f32[512,128]{1,0:T(8,128)}, f32[34,8,128]{2,1,0:T(8,128)}) custom-call(f32[32,2,256]{2,1,0:T(2,128)} %bitcast.17, f32[32,32,128]{2,1,0:T(8,128)} %kap.5, f32[32,32,128]{2,1,0:T(8,128)} %prs.3, f32[128,256]{1,0:T(8,128)} %basis.5), custom_call_target="tpu_custom_call" | custom-call | flops 2000000 | bytes 100000000 | tf_op jit(solution)/shard_map/pack/pallas_call | solution.py:86
  2.9 6.0 %collective-permute-start = (f32[34,8,128]{2,1,0:T(8,128)}, f32[34,8,128]{2,1,0:T(8,128)S(1)}, u32[]{:S(2)}, u32[]{:S(2)}) collective-permute-start(f32[34,8,128]{2,1,0:T(8,128)} %get-tuple-element.13), channel_id=1, source_target_pairs={{0,1},{1,0},{2,3},{3,2},{4,5},{5,4},{6,7},{7,6},{8,9},{9,8},{10,11... | collective-permute-start | bytes 417800 | tf_op jit(solution)/shard_map/ppermute | solution.py:512
  8.9 11.2 %all-to-all-start = ((f32[128,4,128]{2,1,0:T(4,128)}), f32[128,4,128]{2,1,0:T(4,128)S(1)}, u32[]{:S(2)}, u32[]{:S(2)}) async-start(f32[128,4,128]{2,1,0:T(4,128)} %bitcast.16), calls=%async_computation | async-start | bytes 524288 | tf_op jit(solution)/shard_map/all_to_all | solution.py:504
  20.1 0.0 collective-permute-done.beside.strip
  20.2 0.0 copy-start.2
  20.2 1.2 fusion
  21.4 2.3 %collective-permute-start.1 = (f32[3,32,4,128]{3,2,1,0:T(4,128)S(1)}, f32[3,32,4,128]{3,2,1,0:T(4,128)S(1)}, u32[]{:S(2)}, u32[]{:S(2)}) collective-permute-start(f32[3,32,4,128]{3,2,1,0:T(4,128)S(1)} %get-tuple-element.20), channel_id=1, source_target_pairs={{2,0},{4,2},{6,4},{8,6},{10,8},{12,10},{14,12},{16,14},{18,16},{20... | collective-permute-start | bytes 589832 | tf_op jit(solution)/shard_map/ppermute | solution.py:516
  23.7 3.3 %collective-permute-start.2 = (f32[3,32,4,128]{3,2,1,0:T(4,128)S(1)}, f32[3,32,4,128]{3,2,1,0:T(4,128)S(1)}, u32[]{:S(2)}, u32[]{:S(2)}) collective-permute-start(f32[3,32,4,128]{3,2,1,0:T(4,128)S(1)} %get-tuple-element.19), channel_id=1, source_target_pairs={{0,2},{2,4},{4,6},{6,8},{8,10},{10,12},{12,14},{14,16},{16,18},{18... | collective-permute-start | bytes 589832 | tf_op jit(solution)/shard_map/ppermute | solution.py:517
  27.0 5.5 %all-to-all-done = f32[128,4,128]{2,1,0:T(4,128)S(1)} async-done(((f32[128,4,128]{2,1,0:T(4,128)}), f32[128,4,128]{2,1,0:T(4,128)S(1)}, u32[]{:S(2)}, u32[]{:S(2)}) %all-to-all-start) | async-done | bytes 262176 | tf_op jit(solution)/shard_map/all_to_all | solution.py:504
  32.5 0.0 copy-start.6
  32.5 0.0 copy-done.2
  32.5 0.7 copy-done.6
  33.2 4.6 %expand.1 = f32[32,48,128]{2,1,0:T(8,128)} custom-call(f32[512,128]{1,0:T(8,128)} %bitcast.15, f32[128,256]{1,0:T(8,128)} %basis.5, f32[34,8,128]{2,1,0:T(8,128)} %copy-done.2, f32[4096,256]{1,0:T(8,128)} %first_basis.3), custom_call_target="tpu_custom_call" | custom-call | flops 1056964608 | bytes 40000000 | tf_op jit(solution)/shard_map/expand/pallas_call | solution.py:157
  37.8 0.0 collective-permute-done.1.upper
  37.8 0.0 collective-permute-done.2.lower
  37.9 4.0 %all-to-all-start.1 = ((f32[32,48,128]{2,1,0:T(8,128)}), f32[32,48,128]{2,1,0:T(8,128)S(1)}, u32[]{:S(2)}, u32[]{:S(2)}) async-start(f32[32,48,128]{2,1,0:T(8,128)} %expand.1), calls=%async_computation.1 | async-start | bytes 1572864 | tf_op jit(solution)/shard_map/all_to_all | solution.py:504
  41.9 0.0 copy-done.8
  41.9 0.1 copy.7.basis_z
  41.9 0.0 copy-done
  41.9 0.0 copy-done.1
  41.9 0.0 copy-start.3
  41.9 0.9 copy-done.3
  42.9 0.0 copy-start.4
  42.9 0.0 copy-start.7
  42.9 4.9 %statics.1 = (f32[14,32,40,128]{3,2,1,0:T(8,128)}, f32[1024,256]{1,0:T(8,128)}) custom-call(f32[32,32,128]{2,1,0:T(8,128)S(1)} %copy-done, f32[32,32,128]{2,1,0:T(8,128)S(1)} %copy-done.1, f32[3,32,4,128]{3,2,1,0:T(4,128)S(1)} %collective-permute-done.1.upper, f32[3,32,4,128]{3,2,1,0:T(4,128)S(1)} %collective-permute-done.2.lower, ...), custom_call_target="tpu_custom_call" | custom-call | flops 20000000 | bytes 150000000 | tf_op jit(solution)/shard_map/statics/pallas_call | solution.py:281
  47.8 0.0 copy-start.5
  47.8 8.3 %all-to-all-done.1.layers = f32[32,48,128]{2,1,0:T(8,128)S(1)} async-done(((f32[32,48,128]{2,1,0:T(8,128)}), f32[32,48,128]{2,1,0:T(8,128)S(1)}, u32[]{:S(2)}, u32[]{:S(2)}) %all-to-all-start.1) | async-done | bytes 786464 | tf_op jit(solution)/shard_map/all_to_all | solution.py:504
  56.2 18.0 %on_grid.1 = f32[32,32,128]{2,1,0:T(8,128)S(1)} custom-call(f32[32,16]{1,0:T(8,128)S(1)} %copy.7.basis_z, f32[32,48,128]{2,1,0:T(8,128)S(1)} %all-to-all-done.1.layers, f32[32,32,128]{2,1,0:T(8,128)S(1)} %copy-done, f32[14,32,40,128]{3,2,1,0:T(8,128)} %get-tuple-element.17.fields), custom_call_target="tpu_custom_call" | custom-call | flops 100000000 | bytes 12000000 | tf_op jit(solution)/shard_map/on_grid/pallas_call | solution.py:454
  74.2 15.2 %all_to_all.25 = f32[32,32,128]{2,1,0:T(8,128)S(1)} all-to-all(f32[32,32,128]{2,1,0:T(8,128)S(1)} %on_grid.1), channel_id=1, replica_groups=mesh['y'=4,'zl'=4,'x'=4,'core'=2,'zh'=2] {'y','x','core'}, dimensions={0} | all-to-all | bytes 1048576 | tf_op jit(solution)/shard_map/all_to_all | solution.py:504
  89.3 0.0 copy-done.4
  89.3 0.0 copy-done.5
  89.3 1.7 %project.1 = f32[8,64,128]{2,1,0:T(8,128)S(1)} custom-call(f32[1024,128]{1,0:T(8,128)S(1)} %bitcast.14, f32[128,256]{1,0:T(8,128)S(1)} %copy-done.4, f32[1024,256]{1,0:T(8,128)S(1)} %copy-done.5), custom_call_target="tpu_custom_call" | custom-call | flops 503316480 | bytes 2000000 | tf_op jit(solution)/shard_map/project/pallas_call | solution.py:490
  91.0 17.6 %all_to_all.26 = f32[8,64,128]{2,1,0:T(8,128)S(1)} all-to-all(f32[8,64,128]{2,1,0:T(8,128)S(1)} %project.1), channel_id=1, replica_groups=mesh['y'=4,'zl'=4,'x'=4,'core'=2,'zh'=2] {'zl','zh'}, dimensions={0} | all-to-all | bytes 524288 | tf_op jit(solution)/shard_map/all_to_all | solution.py:504
  108.6 0.6 reduce_sum.9
  109.2 4.0 %all-to-all-start.4 = ((f32[32,2,128]{2,1,0:T(2,128)}), f32[32,2,128]{2,1,0:T(2,128)S(1)}, u32[]{:S(2)}, u32[]{:S(2)}) async-start(f32[32,2,128]{2,1,0:T(2,128)} %bitcast.8), calls=%async_computation.4 | async-start | bytes 65536 | tf_op jit(solution)/shard_map/all_to_all | solution.py:504
  113.2 7.4 %all-to-all-done.4 = f32[32,2,128]{2,1,0:T(2,128)S(1)} async-done(((f32[32,2,128]{2,1,0:T(2,128)}), f32[32,2,128]{2,1,0:T(2,128)S(1)}, u32[]{:S(2)}, u32[]{:S(2)}) %all-to-all-start.4) | async-done | bytes 32800 | tf_op jit(solution)/shard_map/all_to_all | solution.py:504
  120.6 0.0 copy-done.7
  120.6 0.6 dynamic-slice_add_fusion
  (1 shorter events, 0.0 us)
Async XLA Ops:
  0.0 41.9 %copy-start = (f32[32,32,128]{2,1,0:T(8,128)S(1)}, f32[32,32,128]{2,1,0:T(8,128)}, u32[]{:S(2)}) copy-start(f32[32,32,128]{2,1,0:T(8,128)} %kap.5) | copy-start | bytes 1572868
  0.0 41.9 %copy-start.1 = (f32[32,32,128]{2,1,0:T(8,128)S(1)}, f32[32,32,128]{2,1,0:T(8,128)}, u32[]{:S(2)}) copy-start(f32[32,32,128]{2,1,0:T(8,128)} %prs.3) | copy-start | bytes 1572868
  0.0 41.9 %copy-start.8 = (f32[32,16]{0,1:T(8,128)S(1)}, f32[32,16]{0,1:T(8,128)}, u32[]{:S(2)}) copy-start(f32[32,16]{0,1:T(8,128)} %param.9) | copy-start | bytes 6148
  2.9 17.3 %collective-permute-start = (f32[34,8,128]{2,1,0:T(8,128)}, f32[34,8,128]{2,1,0:T(8,128)S(1)}, u32[]{:S(2)}, u32[]{:S(2)}) collective-permute-start(f32[34,8,128]{2,1,0:T(8,128)} %get-tuple-element.13), channel_id=1, source_target_pairs={{0,1},{1,0},{2,3},{3,2},{4,5},{5,4},{6,7},{7,6},{8,9},{9,8},{10,11... | collective-permute-start | bytes 417800 | tf_op jit(solution)/shard_map/ppermute | solution.py:512
  8.9 23.6 %all-to-all-start = ((f32[128,4,128]{2,1,0:T(4,128)}), f32[128,4,128]{2,1,0:T(4,128)S(1)}, u32[]{:S(2)}, u32[]{:S(2)}) async-start(f32[128,4,128]{2,1,0:T(4,128)} %bitcast.16), calls=%async_computation | async-start | bytes 524288 | tf_op jit(solution)/shard_map/all_to_all | solution.py:504
  20.2 12.3 %copy-start.2 = (f32[34,8,128]{2,1,0:T(8,128)}, f32[34,8,128]{2,1,0:T(8,128)S(1)}, u32[]{:S(2)}) copy-start(f32[34,8,128]{2,1,0:T(8,128)S(1)} %collective-permute-done.beside.strip) | copy-start | bytes 417796
  21.4 16.4 %collective-permute-start.1 = (f32[3,32,4,128]{3,2,1,0:T(4,128)S(1)}, f32[3,32,4,128]{3,2,1,0:T(4,128)S(1)}, u32[]{:S(2)}, u32[]{:S(2)}) collective-permute-start(f32[3,32,4,128]{3,2,1,0:T(4,128)S(1)} %get-tuple-element.20), channel_id=1, source_target_pairs={{2,0},{4,2},{6,4},{8,6},{10,8},{12,10},{14,12},{16,14},{18,16},{20... | collective-permute-start | bytes 589832 | tf_op jit(solution)/shard_map/ppermute | solution.py:516
  23.7 14.2 %collective-permute-start.2 = (f32[3,32,4,128]{3,2,1,0:T(4,128)S(1)}, f32[3,32,4,128]{3,2,1,0:T(4,128)S(1)}, u32[]{:S(2)}, u32[]{:S(2)}) collective-permute-start(f32[3,32,4,128]{3,2,1,0:T(4,128)S(1)} %get-tuple-element.19), channel_id=1, source_target_pairs={{0,2},{2,4},{4,6},{6,8},{8,10},{10,12},{12,14},{14,16},{16,18},{18... | collective-permute-start | bytes 589832 | tf_op jit(solution)/shard_map/ppermute | solution.py:517
  32.5 0.7 copy-start.6
  37.9 18.3 %all-to-all-start.1 = ((f32[32,48,128]{2,1,0:T(8,128)}), f32[32,48,128]{2,1,0:T(8,128)S(1)}, u32[]{:S(2)}, u32[]{:S(2)}) async-start(f32[32,48,128]{2,1,0:T(8,128)} %expand.1), calls=%async_computation.1 | async-start | bytes 1572864 | tf_op jit(solution)/shard_map/all_to_all | solution.py:504
  41.9 0.9 copy-start.3
  42.9 46.5 %copy-start.4 = (f32[128,256]{1,0:T(8,128)S(1)}, f32[128,256]{1,0:T(8,128)}, u32[]{:S(2)}) copy-start(f32[128,256]{1,0:T(8,128)} %basis.5) | copy-start | bytes 393220
  42.9 77.7 %copy-start.7 = (f32[2,16,2,256]{3,2,1,0:T(2,128)S(1)}, f32[2,16,2,256]{3,2,1,0:T(2,128)}, u32[]{:S(2)}) copy-start(f32[2,16,2,256]{3,2,1,0:T(2,128)} %param.6) | copy-start | bytes 196612
  47.8 41.5 %copy-start.5 = (f32[1024,256]{1,0:T(8,128)S(1)}, f32[1024,256]{1,0:T(8,128)}, u32[]{:S(2)}) copy-start(f32[1024,256]{1,0:T(8,128)} %get-tuple-element.18.plane_rows) | copy-start | bytes 3145732
  109.2 11.4 %all-to-all-start.4 = ((f32[32,2,128]{2,1,0:T(2,128)}), f32[32,2,128]{2,1,0:T(2,128)S(1)}, u32[]{:S(2)}, u32[]{:S(2)}) async-start(f32[32,2,128]{2,1,0:T(2,128)} %bitcast.8), calls=%async_computation.4 | async-start | bytes 65536 | tf_op jit(solution)/shard_map/all_to_all | solution.py:504

commit v5 on v4

--- a/solution.py
+++ b/solution.py
@@ -516,7 +516,6 @@
     upper = lax.ppermute(heads, GX, [(i + 1, i) for i in range(127)])
     lower = lax.ppermute(tails, GX, [(i, i + 1) for i in range(127)])
     message = expand(gathered.reshape(512, COLS), basis_y, strip, first_axis_basis)
-    message, upper, lower = lax.optimization_barrier((message, upper, lower))
     fields, plane_rows = statics(conductivity, pressure, upper, lower, strip, first_axis_basis)
     layers = exchanged(message, PLANE)
     modes = on_grid(basis_z, layers, conductivity, fields)

time: 122 us -> 132 us (1.082)
  blocking collectives: 32.7 us -> 39.4 us
  starting transfers between devices: 30.8 us -> 34.1 us
    all_to_all x3, waiting for transfers between devices: 21.2 us -> 7.97 us  [exchanged(): return lax.all_to_all(values, axes, split_axis=0, concat_axis=0, tiled=True)]
    ppermute x1, waiting for transfers between devices: 0.01 us -> 7.72 us  [per_device(): strip = lax.ppermute(strip, 'zh', [(0, 1), (1, 0)])]
    all_to_all x2, blocking collectives: 32.7 us -> 39.4 us  [exchanged(): return lax.all_to_all(values, axes, split_axis=0, concat_axis=0, tiled=True)]
    ppermute x1, waiting for transfers between devices: 0.01 us -> 6.47 us  [per_device(): upper = lax.ppermute(heads, GX, [(i + 1, i) for i in range(127)])]
    all_to_all x3, starting transfers between devices: 19.2 us -> 24.3 us  [exchanged(): return lax.all_to_all(values, axes, split_axis=0, concat_axis=0, tiled=True)]
    ppermute x1, starting transfers between devices: 6.01 us -> 4.3 us  [per_device(): strip = lax.ppermute(strip, 'zh', [(0, 1), (1, 0)])]
  transfers between devices with their start and end apart: 6 -> 6, of which waited for: 3 -> 4; matrix products, arithmetic and copies ran while one was open for 1% -> 1% of each run, Pallas kernels for 8% -> 4%
where the time goes in v5:
time: 132 us; the launch traced here: 131 us
  blocking collectives  39.4 us (30%)
  starting transfers between devices  34.1 us (26%)
  Pallas kernels  31.5 us (24%)
  waiting for transfers between devices  22.2 us (17%)
  local copies, waits for them, and re-layouts  2.7 us (2%)
  other arithmetic  1.35 us (1%)
    all_to_all x2, blocking collectives, exchanged(): return lax.all_to_all(values, axes, split_axis=0, concat_axis=0, tiled=True)  39.4 us
    all_to_all x3, starting transfers between devices, exchanged(): return lax.all_to_all(values, axes, split_axis=0, concat_axis=0, tiled=True)  24.3 us
    pallas_call x1, Pallas kernels, on_grid(): pl.pallas_call(grid_kernel, out_shape=jax.ShapeDtypeStruct((DIRECTIONS *...  17.4 us
    all_to_all x3, waiting for transfers between devices, exchanged(): return lax.all_to_all(values, axes, split_axis=0, concat_axis=0, tiled=True)  7.97 us
    ppermute x1, waiting for transfers between devices, per_device(): strip = lax.ppermute(strip, 'zh', [(0, 1), (1, 0)])  7.72 us
    ppermute x1, waiting for transfers between devices, per_device(): upper = lax.ppermute(heads, GX, [(i + 1, i) for i in range(127)])  6.47 us
    pallas_call x1, Pallas kernels, statics(): pl.pallas_call(statics_kernel, out_shape=(jax.ShapeDtypeStruct((FIELDS,)...  4.93 us
    pallas_call x1, Pallas kernels, expand(): pl.pallas_call(expand_kernel, out_shape=jax.ShapeDtypeStruct((32, EXT_ROW...  4.64 us
  transfers between devices with their start and end apart: 6, of which 4 were waited for; matrix products, arithmetic and copies ran while one was open for 1% of the time, Pallas kernels for 4%

profile of v5, /device:TPU:33, one launch (start us, length us, event | category | flops | bytes accessed | tf_op | source)
XLA Modules:
  0.0 131.4 jit_solution(18025256952260280917)
XLA Ops:
  0.0 0.0 copy-start
  0.0 0.0 copy-start.1
  0.0 0.0 copy-start.8
  0.0 2.9 %pack.1 = (f32[512,128]{1,0:T(8,128)}, f32[34,8,128]{2,1,0:T(8,128)}) custom-call(f32[32,2,256]{2,1,0:T(2,128)} %bitcast.17, f32[32,32,128]{2,1,0:T(8,128)} %kap.5, f32[32,32,128]{2,1,0:T(8,128)} %prs.3, f32[128,256]{1,0:T(8,128)} %basis.5), custom_call_target="tpu_custom_call" | custom-call | flops 2000000 | bytes 100000000 | tf_op jit(solution)/shard_map/pack/pallas_call | solution.py:86
  2.9 12.8 %all-to-all-start = ((f32[128,4,128]{2,1,0:T(4,128)}), f32[128,4,128]{2,1,0:T(4,128)S(1)}, u32[]{:S(2)}, u32[]{:S(2)}) async-start(f32[128,4,128]{2,1,0:T(4,128)} %bitcast.16), calls=%async_computation | async-start | bytes 524288 | tf_op jit(solution)/shard_map/all_to_all | solution.py:504
  15.6 4.3 %collective-permute-start = (f32[34,8,128]{2,1,0:T(8,128)}, f32[34,8,128]{2,1,0:T(8,128)S(1)}, u32[]{:S(2)}, u32[]{:S(2)}) collective-permute-start(f32[34,8,128]{2,1,0:T(8,128)} %get-tuple-element.10), channel_id=1, source_target_pairs={{0,1},{1,0},{2,3},{3,2},{4,5},{5,4},{6,7},{7,6},{8,9},{9,8},{10,11... | collective-permute-start | bytes 417800 | tf_op jit(solution)/shard_map/ppermute | solution.py:512
  19.9 7.7 %collective-permute-done.beside.strip = f32[34,8,128]{2,1,0:T(8,128)S(1)} collective-permute-done((f32[34,8,128]{2,1,0:T(8,128)}, f32[34,8,128]{2,1,0:T(8,128)S(1)}, u32[]{:S(2)}, u32[]{:S(2)}) %collective-permute-start) | collective-permute-done | bytes 139296 | tf_op jit(solution)/shard_map/ppermute | solution.py:512
  27.7 0.0 copy-start.2
  27.7 0.6 all-to-all-done
  28.3 0.0 copy-start.6
  28.3 0.0 copy-done.2
  28.3 0.7 copy-done.6
  29.0 4.6 %expand.1 = f32[32,48,128]{2,1,0:T(8,128)} custom-call(f32[512,128]{1,0:T(8,128)} %bitcast.15, f32[128,256]{1,0:T(8,128)} %basis.5, f32[34,8,128]{2,1,0:T(8,128)} %copy-done.2, f32[4096,256]{1,0:T(8,128)} %first_basis.3), custom_call_target="tpu_custom_call" | custom-call | flops 1056964608 | bytes 40000000 | tf_op jit(solution)/shard_map/expand/pallas_call | solution.py:157
  33.6 7.5 %all-to-all-start.1 = ((f32[32,48,128]{2,1,0:T(8,128)}), f32[32,48,128]{2,1,0:T(8,128)S(1)}, u32[]{:S(2)}, u32[]{:S(2)}) async-start(f32[32,48,128]{2,1,0:T(8,128)} %expand.1), calls=%async_computation.1 | async-start | bytes 1572864 | tf_op jit(solution)/shard_map/all_to_all | solution.py:504
  41.1 1.0 slice_bitcast_fusion
  42.1 0.0 copy-done
  42.1 0.0 copy-done.1
  42.2 0.0 copy-start.4
  42.2 0.1 fusion
  42.3 2.1 %collective-permute-start.1 = (f32[3,32,4,128]{3,2,1,0:T(4,128)S(1)}, f32[3,32,4,128]{3,2,1,0:T(4,128)S(1)}, u32[]{:S(2)}, u32[]{:S(2)}) collective-permute-start(f32[3,32,4,128]{3,2,1,0:T(4,128)S(1)} %get-tuple-element.14), channel_id=1, source_target_pairs={{2,0},{4,2},{6,4},{8,6},{10,8},{12,10},{14,12},{16,14},{18,16},{20... | collective-permute-start | bytes 589832 | tf_op jit(solution)/shard_map/ppermute | solution.py:516
  44.4 3.4 %collective-permute-start.2 = (f32[3,32,4,128]{3,2,1,0:T(4,128)S(1)}, f32[3,32,4,128]{3,2,1,0:T(4,128)S(1)}, u32[]{:S(2)}, u32[]{:S(2)}) collective-permute-start(f32[3,32,4,128]{3,2,1,0:T(4,128)S(1)} %get-tuple-element.13), channel_id=1, source_target_pairs={{0,2},{2,4},{4,6},{6,8},{8,10},{10,12},{12,14},{14,16},{16,18},{18... | collective-permute-start | bytes 589832 | tf_op jit(solution)/shard_map/ppermute | solution.py:517
  47.8 0.0 copy-done.8
  47.8 0.1 copy.7.basis_z
  47.9 6.5 %collective-permute-done.1.upper = f32[3,32,4,128]{3,2,1,0:T(4,128)S(1)} collective-permute-done((f32[3,32,4,128]{3,2,1,0:T(4,128)S(1)}, f32[3,32,4,128]{3,2,1,0:T(4,128)S(1)}, u32[]{:S(2)}, u32[]{:S(2)}) %collective-permute-start.1) | collective-permute-done | bytes 196640 | tf_op jit(solution)/shard_map/ppermute | solution.py:516
  54.4 0.0 collective-permute-done.2.lower
  54.4 0.0 copy-start.3
  54.4 0.9 copy-done.3
  55.3 0.0 copy-start.7
  55.3 4.9 %statics.1 = (f32[14,32,40,128]{3,2,1,0:T(8,128)}, f32[1024,256]{1,0:T(8,128)}) custom-call(f32[32,32,128]{2,1,0:T(8,128)S(1)} %copy-done, f32[32,32,128]{2,1,0:T(8,128)S(1)} %copy-done.1, f32[3,32,4,128]{3,2,1,0:T(4,128)S(1)} %collective-permute-done.1.upper, f32[3,32,4,128]{3,2,1,0:T(4,128)S(1)} %collective-permute-done.2.lower, ...), custom_call_target="tpu_custom_call" | custom-call | flops 20000000 | bytes 150000000 | tf_op jit(solution)/shard_map/statics/pallas_call | solution.py:281
  60.2 0.0 copy-start.5
  60.3 0.0 all-to-all-done.1.layers
  60.3 17.4 %on_grid.1 = f32[32,32,128]{2,1,0:T(8,128)S(1)} custom-call(f32[32,16]{1,0:T(8,128)S(1)} %copy.7.basis_z, f32[32,48,128]{2,1,0:T(8,128)S(1)} %all-to-all-done.1.layers, f32[32,32,128]{2,1,0:T(8,128)S(1)} %copy-done, f32[14,32,40,128]{3,2,1,0:T(8,128)} %get-tuple-element.11.fields), custom_call_target="tpu_custom_call" | custom-call | flops 100000000 | bytes 12000000 | tf_op jit(solution)/shard_map/on_grid/pallas_call | solution.py:454
  77.7 20.8 %all_to_all.25 = f32[32,32,128]{2,1,0:T(8,128)S(1)} all-to-all(f32[32,32,128]{2,1,0:T(8,128)S(1)} %on_grid.1), channel_id=1, replica_groups=mesh['y'=4,'zl'=4,'x'=4,'core'=2,'zh'=2] {'y','x','core'}, dimensions={0} | all-to-all | bytes 1048576 | tf_op jit(solution)/shard_map/all_to_all | solution.py:504
  98.5 0.0 copy-done.4
  98.5 0.0 copy-done.5
  98.5 1.7 %project.1 = f32[8,64,128]{2,1,0:T(8,128)S(1)} custom-call(f32[1024,128]{1,0:T(8,128)S(1)} %bitcast.14, f32[128,256]{1,0:T(8,128)S(1)} %copy-done.4, f32[1024,256]{1,0:T(8,128)S(1)} %copy-done.5), custom_call_target="tpu_custom_call" | custom-call | flops 503316480 | bytes 2000000 | tf_op jit(solution)/shard_map/project/pallas_call | solution.py:490
  100.2 18.6 %all_to_all.26 = f32[8,64,128]{2,1,0:T(8,128)S(1)} all-to-all(f32[8,64,128]{2,1,0:T(8,128)S(1)} %project.1), channel_id=1, replica_groups=mesh['y'=4,'zl'=4,'x'=4,'core'=2,'zh'=2] {'zl','zh'}, dimensions={0} | all-to-all | bytes 524288 | tf_op jit(solution)/shard_map/all_to_all | solution.py:504
  118.8 0.6 reduce_sum.9
  119.4 4.0 %all-to-all-start.4 = ((f32[32,2,128]{2,1,0:T(2,128)}), f32[32,2,128]{2,1,0:T(2,128)S(1)}, u32[]{:S(2)}, u32[]{:S(2)}) async-start(f32[32,2,128]{2,1,0:T(2,128)} %bitcast.8), calls=%async_computation.4 | async-start | bytes 65536 | tf_op jit(solution)/shard_map/all_to_all | solution.py:504
  123.4 7.4 %all-to-all-done.4 = f32[32,2,128]{2,1,0:T(2,128)S(1)} async-done(((f32[32,2,128]{2,1,0:T(2,128)}), f32[32,2,128]{2,1,0:T(2,128)S(1)}, u32[]{:S(2)}, u32[]{:S(2)}) %all-to-all-start.4) | async-done | bytes 32800 | tf_op jit(solution)/shard_map/all_to_all | solution.py:504
  130.8 0.0 copy-done.7
  130.8 0.6 dynamic-slice_add_fusion
Async XLA Ops:
  0.0 42.1 %copy-start = (f32[32,32,128]{2,1,0:T(8,128)S(1)}, f32[32,32,128]{2,1,0:T(8,128)}, u32[]{:S(2)}) copy-start(f32[32,32,128]{2,1,0:T(8,128)} %kap.5) | copy-start | bytes 1572868
  0.0 42.1 %copy-start.1 = (f32[32,32,128]{2,1,0:T(8,128)S(1)}, f32[32,32,128]{2,1,0:T(8,128)}, u32[]{:S(2)}) copy-start(f32[32,32,128]{2,1,0:T(8,128)} %prs.3) | copy-start | bytes 1572868
  0.0 47.8 %copy-start.8 = (f32[32,16]{0,1:T(8,128)S(1)}, f32[32,16]{0,1:T(8,128)}, u32[]{:S(2)}) copy-start(f32[32,16]{0,1:T(8,128)} %param.9) | copy-start | bytes 6148
  2.9 25.4 %all-to-all-start = ((f32[128,4,128]{2,1,0:T(4,128)}), f32[128,4,128]{2,1,0:T(4,128)S(1)}, u32[]{:S(2)}, u32[]{:S(2)}) async-start(f32[128,4,128]{2,1,0:T(4,128)} %bitcast.16), calls=%async_computation | async-start | bytes 524288 | tf_op jit(solution)/shard_map/all_to_all | solution.py:504
  15.6 12.0 %collective-permute-start = (f32[34,8,128]{2,1,0:T(8,128)}, f32[34,8,128]{2,1,0:T(8,128)S(1)}, u32[]{:S(2)}, u32[]{:S(2)}) collective-permute-start(f32[34,8,128]{2,1,0:T(8,128)} %get-tuple-element.10), channel_id=1, source_target_pairs={{0,1},{1,0},{2,3},{3,2},{4,5},{5,4},{6,7},{7,6},{8,9},{9,8},{10,11... | collective-permute-start | bytes 417800 | tf_op jit(solution)/shard_map/ppermute | solution.py:512
  27.7 0.6 copy-start.2
  28.3 0.7 copy-start.6
  33.6 26.6 %all-to-all-start.1 = ((f32[32,48,128]{2,1,0:T(8,128)}), f32[32,48,128]{2,1,0:T(8,128)S(1)}, u32[]{:S(2)}, u32[]{:S(2)}) async-start(f32[32,48,128]{2,1,0:T(8,128)} %expand.1), calls=%async_computation.1 | async-start | bytes 1572864 | tf_op jit(solution)/shard_map/all_to_all | solution.py:504
  42.2 56.4 %copy-start.4 = (f32[128,256]{1,0:T(8,128)S(1)}, f32[128,256]{1,0:T(8,128)}, u32[]{:S(2)}) copy-start(f32[128,256]{1,0:T(8,128)} %basis.5) | copy-start | bytes 393220
  42.3 12.1 %collective-permute-start.1 = (f32[3,32,4,128]{3,2,1,0:T(4,128)S(1)}, f32[3,32,4,128]{3,2,1,0:T(4,128)S(1)}, u32[]{:S(2)}, u32[]{:S(2)}) collective-permute-start(f32[3,32,4,128]{3,2,1,0:T(4,128)S(1)} %get-tuple-element.14), channel_id=1, source_target_pairs={{2,0},{4,2},{6,4},{8,6},{10,8},{12,10},{14,12},{16,14},{18,16},{20... | collective-permute-start | bytes 589832 | tf_op jit(solution)/shard_map/ppermute | solution.py:516
  44.4 10.0 %collective-permute-start.2 = (f32[3,32,4,128]{3,2,1,0:T(4,128)S(1)}, f32[3,32,4,128]{3,2,1,0:T(4,128)S(1)}, u32[]{:S(2)}, u32[]{:S(2)}) collective-permute-start(f32[3,32,4,128]{3,2,1,0:T(4,128)S(1)} %get-tuple-element.13), channel_id=1, source_target_pairs={{0,2},{2,4},{4,6},{6,8},{8,10},{10,12},{12,14},{14,16},{16,18},{18... | collective-permute-start | bytes 589832 | tf_op jit(solution)/shard_map/ppermute | solution.py:517
  54.4 0.9 copy-start.3
  55.3 75.5 %copy-start.7 = (f32[2,16,2,256]{3,2,1,0:T(2,128)S(1)}, f32[2,16,2,256]{3,2,1,0:T(2,128)}, u32[]{:S(2)}) copy-start(f32[2,16,2,256]{3,2,1,0:T(2,128)} %param.6) | copy-start | bytes 196612
  60.2 38.3 %copy-start.5 = (f32[1024,256]{1,0:T(8,128)S(1)}, f32[1024,256]{1,0:T(8,128)}, u32[]{:S(2)}) copy-start(f32[1024,256]{1,0:T(8,128)} %get-tuple-element.12.plane_rows) | copy-start | bytes 3145732
  119.4 11.4 %all-to-all-start.4 = ((f32[32,2,128]{2,1,0:T(2,128)}), f32[32,2,128]{2,1,0:T(2,128)S(1)}, u32[]{:S(2)}, u32[]{:S(2)}) async-start(f32[32,2,128]{2,1,0:T(2,128)} %bitcast.8), calls=%async_computation.4 | async-start | bytes 65536 | tf_op jit(solution)/shard_map/all_to_all | solution.py:504
